TPU v7x, 256 devices: a whole 4x4x8 slice. The times are simulated.
256 devices in a mesh: section: 4 (over y_hi, core), dp: 64 (over x, y_lo, z).
Axes of the slice: x: 4, y: 4 (y_hi: 2, y_lo: 2; y = y_hi * 2 + y_lo), z: 8, core: 2. Of those that a mesh axis runs over, the one named last changes fastest.
Arguments:
- activations: bfloat16 [4, 16384, 8192], P('section', 'dp'), may hold values from -600 to 600, as said below
- tail_grads: bfloat16 [4, 16384, 512], P('section', 'dp'), may hold values from -48 to 48, as said below
- tail_slots: int32 [4, 64, 4], P('section', 'dp'), may hold values from 0 to 3, each once within a row
- master: float32 [4, 8192, 512], P('section', 'dp'), may hold values from -6 to 6
- moment1: float32 [4, 8192, 512], P('section', 'dp'), may hold values from -0.00029296876 to 0.00029296876
- moment2: float32 [4, 8192, 512], P('section', 'dp'), may hold values from 1.1920929e-09 to 2.9802322e-08
- overflow: int32 [4, 64], P('section', 'dp'), may hold values from 0 to 1, as said below
- clip_on: int32 [4], P('section'), may hold values from 0 to 1, as said below
- next_inputs: bfloat16 [4, 2048, 8192], P('section', 'dp'), may hold values from -6 to 6
Outputs:
- new_master: float32 [4, 8192, 512], P('section', 'dp')
- next_out: bfloat16 [4, 2048, 512], P('section', 'dp')
Inputs may be any that keep to these rules, and one draw needn't show every extreme that they name: `tail_slots`: each row along the last dimension names every slot once. `overflow`: at least one shard is flagged and at least one is not. `clip_on`: at least one section is clipped and at least one is not. `activations`: real-valued. `tail_grads`: real-valued.
All inputs are finite; a program needn't handle non-finite values.
Results may differ from a plain program's by a relative error of at most 0.0049.
Values may be sent and summed in bfloat16 or wider, within the bound.
No kernel may reach another device: no remote copies, remote signals or barrier semaphores. Data moves between devices by JAX's collectives and lax.ppermute only.
A program may use at most 64 MiB of HBM per device.

v0:
```python
import functools
import math

import jax
import jax.numpy as jnp
from jax import lax
from jax.sharding import Mesh
from jax.sharding import PartitionSpec as P

DP = ("dp_0", "dp_1", "dp_2")
SECTION_DP = ("section_0", "section_1", "dp_0", "dp_1", "dp_2")
SECTION = ("section_0", "section_1")


beta_one = 0.9
beta_two = 0.95
correct_one = 1.0 - 0.9**20
correct_two = 1.0 - 0.95**20
adam_eps = 1e-08
decay_rate = 0.1
learn_rate = 0.1


def one_axis_at_a_time(x, axes):
    return functools.reduce(lax.psum, axes, x)


def in_order(tiles, dim):
    tiles = jnp.moveaxis(tiles, 0, dim)
    shape = tiles.shape
    return tiles.reshape(*shape[:dim], shape[dim] * shape[dim + 1], *shape[dim + 2 :])


def all_blocks(x, axes, sequence):
    tiles = x
    for k in sequence:
        tiles = lax.all_gather(tiles, axes[k])
    done = sequence[::-1]
    back = [done.index(k) for k in range(len(axes))]
    tiles = tiles.transpose(*back, *range(len(axes), tiles.ndim))
    return tiles.reshape(-1, *x.shape)


def gathered_by_axis(x, axes, sequence, dim):
    return in_order(all_blocks(x, axes, sequence), dim)


def local(
    activations, tail_grads, tail_slots, master, moment1, moment2, overflow, clip_on, next_inputs
):
    stashed = activations[0]
    local_tails = tail_grads[0]
    slots = tail_slots[0, 0]
    tail_count = slots.shape[0]
    tok_dev, width = stashed.shape
    slab_cols = local_tails.shape[1]
    dp_count = lax.axis_size(DP)
    onehot = (slots[:, None] == jnp.arange(tail_count, dtype=jnp.int32)[None, :]).astype(
        jnp.float32
    )
    shaped = local_tails.reshape(tail_count, tok_dev // tail_count, slab_cols).astype(jnp.float32)
    paired = (
        jnp.einsum("tk,tnc->knc", onehot, shaped).astype(jnp.bfloat16).reshape(tok_dev, slab_cols)
    )
    contract = (((0,), (0,)), ((), ()))
    block = stashed
    summed = lax.psum_scatter(
        lax.dot_general(block, paired, contract, preferred_element_type=jnp.float32),
        DP,
        scatter_dimension=0,
        tiled=True,
    )
    gradient = summed * (1.0 / (tok_dev * dp_count))
    keep = (overflow[0, 0] == 0).astype(jnp.float32)
    partial_sq = keep * jnp.sum(gradient * gradient)
    sumsq = one_axis_at_a_time(partial_sq, SECTION_DP)
    norm_value = jnp.sqrt(sumsq)
    factor = jnp.where(clip_on[0] == 1, 1.0 / jnp.maximum(norm_value, 1.0), 1.0)
    clipped = gradient * factor
    old_master = master[0]
    m_next = beta_one * moment1[0] + (1.0 - beta_one) * clipped
    v_next = beta_two * moment2[0] + (1.0 - beta_two) * (clipped * clipped)
    update = (
        m_next / correct_one / (jnp.sqrt(v_next / correct_two) + adam_eps) + decay_rate * old_master
    )
    updated = jnp.where(keep > 0.5, old_master - learn_rate * update, old_master)
    weights = updated.astype(jnp.bfloat16)
    inputs = next_inputs[0]
    block = inputs
    result = jnp.dot(
        block, gathered_by_axis(weights, DP, (1, 0, 2), 0), preferred_element_type=jnp.float32
    )
    next_out = (result * (1.0 / math.sqrt(width))).astype(jnp.bfloat16)
    return (updated[None], next_out[None])


def solution(mesh):
    finer = Mesh(
        mesh.devices.reshape(2, 2, 4, 2, 8), ("section_0", "section_1", "dp_0", "dp_1", "dp_2")
    )
    return jax.shard_map(
        local,
        mesh=finer,
        in_specs=(
            P(SECTION, DP, None),
            P(SECTION, DP, None),
            P(SECTION, DP, None),
            P(SECTION, DP, None),
            P(SECTION, DP, None),
            P(SECTION, DP, None),
            P(SECTION, DP),
            P(SECTION),
            P(SECTION, DP, None),
        ),
        out_specs=(P(SECTION, DP, None), P(SECTION, DP, None)),
        check_vma=False,
    )
```

profile of v0, /device:TPU:1, one launch (start us, length us, event | category | flops | bytes accessed | tf_op | source)
XLA Modules:
  0.0 570.4 jit_solution(14773777321939710195)
XLA Ops:
  7.2 0.0 reduce-scatter.2.cloned.1.call-start
  7.2 1.3 convolution_convert_fusion
  8.6 10.3 %convolution_bitcast_fusion = f32[8192,512]{0,1:T(8,128)} fusion(bf16[256,512]{1,0:T(8,128)(2,1)S(1)} %bitcast.64, bf16[1,256,8192]{2,1,0:T(8,128)(2,1)} %param.9), kind=kOutput, calls=%fused_computation | convolution fusion | flops 2147483648 | bytes 21233664 | tf_op jit(solution)/shard_map/dot_general | solution.py:68
  18.9 0.0 reduce-scatter.2.cloned.1.call-update
  18.9 0.0 all-gather.6.cloned.1.call-start
  20.3 309.5 %reduce-scatter.2.cloned.1.call-done = f32[128,512]{0,1:T(8,128)} async-done(((f32[8192,512]{0,1:T(8,128)}), f32[128,512]{0,1:T(8,128)}) %reduce-scatter.2.cloned.1.call-update) | async-done | bytes 262160 | tf_op jit(solution)/shard_map/reduce_scatter | solution.py:67
  329.8 1.6 multiply_reduce_fusion
  332.1 0.1 copy.30
  332.3 6.2 %psum.35 = f32[]{:T(128)} all-reduce(f32[]{:T(128)S(6)} %mul.69), channel_id=1, replica_groups=mesh['section_0'=2,'section_1'=2,'dp_0'=4,'dp_1'=2,'dp_2'=8] {'section_0'}, use_global_device_ids=true, to_apply=%region_2.0 | all-reduce | flops 1 | bytes 8 | tf_op jit(solution)/shard_map/psum | solution.py:25
  338.4 0.1 copy.31
  338.6 55.9 %psum.36 = f32[]{:T(128)} all-reduce(f32[]{:T(128)} %psum.35), channel_id=1, replica_groups=mesh['section_0'=2,'section_1'=2,'dp_0'=4,'dp_1'=2,'dp_2'=8] {'section_1'}, use_global_device_ids=true, to_apply=%region_3.0 | all-reduce | flops 1 | bytes 8 | tf_op jit(solution)/shard_map/psum | solution.py:25
  394.5 0.1 copy.34
  394.6 6.7 %psum.37 = f32[]{:T(128)} all-reduce(f32[]{:T(128)} %psum.36), channel_id=1, replica_groups=mesh['section_0'=2,'section_1'=2,'dp_0'=4,'dp_1'=2,'dp_2'=8] {'dp_0'}, use_global_device_ids=true, to_apply=%region_4.0 | all-reduce | flops 1 | bytes 8 | tf_op jit(solution)/shard_map/psum | solution.py:25
  401.4 4.4 psum.38
  405.7 11.3 %psum.39 = f32[]{:T(128)} all-reduce(f32[]{:T(128)} %psum.38), channel_id=1, replica_groups=mesh['section_0'=2,'section_1'=2,'dp_0'=4,'dp_1'=2,'dp_2'=8] {'dp_2'}, use_global_device_ids=true, to_apply=%region_6.0 | all-reduce | flops 1 | bytes 8 | tf_op jit(solution)/shard_map/psum | solution.py:25
  417.8 1.2 fusion.15
  419.0 4.5 all-gather
  423.5 0.8 copy.38
  424.3 0.0 all-gather.8.cloned.1.call-start
  424.4 28.2 %all-gather.6.cloned.1.call-done = bf16[8,128,512]{2,1,0:T(8,128)(2,1)} async-done(((bf16[2,128,512]{2,1,0:T(8,128)(2,1)}), bf16[8,128,512]{2,1,0:T(8,128)(2,1)}) %all-gather.6.cloned.1.call-update) | async-done | bytes 1048592 | tf_op jit(solution)/shard_map/all_gather | solution.py:37
  452.6 0.8 copy.37
  453.4 97.3 %all-gather.8.cloned.1.call-done = bf16[32,2,128,512]{3,2,1,0:T(8,128)(2,1)} async-done(((bf16[4,2,128,512]{3,2,1,0:T(8,128)(2,1)}), bf16[32,2,128,512]{3,2,1,0:T(8,128)(2,1)}) %all-gather.8.cloned.1.call-update) | async-done | bytes 8388624 | tf_op jit(solution)/shard_map/all_gather | solution.py:37
  550.8 7.6 %copy.36 = bf16[4,2,8,128,512]{4,3,2,1,0:T(8,128)(2,1)} copy(bf16[4,2,8,128,512]{4,3,1,0,2:T(8,128)(2,1)} %bitcast.60) | data formatting | bytes 16777216 | tf_op jit(solution)/shard_map/transpose | solution.py:40
  558.3 5.5 fusion.2
  (11 shorter events, 0.1 us)
Async XLA Ops:
  7.2 551.2 %copy-start = (bf16[1,32,8192]{2,1,0:T(8,128)(2,1)S(1)}, bf16[1,32,8192]{2,1,0:T(8,128)(2,1)}, u32[]{:S(2)}) copy-start(bf16[1,32,8192]{2,1,0:T(8,128)(2,1)} %param.17) | copy-start | bytes 1572868
  7.2 322.7 %reduce-scatter.2.cloned.1.call-start = ((), (), s32[]{:S(2)}) async-start(), calls=%async_computation.1 | async-start | bytes 17039360 | tf_op jit(solution)/shard_map/reduce_scatter | solution.py:67
  18.9 313.3 %copy-start.1 = (f32[1,128,512]{2,1,0:T(8,128)S(1)}, f32[1,128,512]{2,1,0:T(8,128)}, u32[]{:S(2)}) copy-start(f32[1,128,512]{2,1,0:T(8,128)} %param.12) | copy-start | bytes 786436
  18.9 319.6 %copy-start.2 = (f32[1,128,512]{2,1,0:T(8,128)S(1)}, f32[1,128,512]{2,1,0:T(8,128)}, u32[]{:S(2)}) copy-start(f32[1,128,512]{2,1,0:T(8,128)} %param.13) | copy-start | bytes 786436
  18.9 375.6 %copy-start.3 = (f32[1,128,512]{2,1,0:T(8,128)S(1)}, f32[1,128,512]{2,1,0:T(8,128)}, u32[]{:S(2)}) copy-start(f32[1,128,512]{2,1,0:T(8,128)} %param.14) | copy-start | bytes 786436
  18.9 433.7 %all-gather.6.cloned.1.call-start = ((), (), s32[]{:S(2)}) async-start(), calls=%async_computation.2 | async-start | bytes 1310720 | tf_op jit(solution)/shard_map/all_gather | solution.py:37
  424.3 126.4 %all-gather.8.cloned.1.call-start = ((), (), s32[]{:S(2)}) async-start(), calls=%async_computation.3 | async-start | bytes 9437184 | tf_op jit(solution)/shard_map/all_gather | solution.py:37
Sparse Core Ops, SparseCore 0:
  19.0 310.7 reduce-scatter.1
  424.5 28.0 all-gather.5
  454.3 96.3 all-gather.7
where the time goes:
time: 571 us; the launch traced here: 570 us
  waiting for transfers between devices  435 us (76%)
  blocking collectives  89 us (16%)
  matrix products  17.1 us (3%)
  between operations  16.6 us (3%)
  local copies, waits for them, and re-layouts  9.7 us (2%)
    reduce_scatter x1, waiting for transfers between devices, local(): lax.psum_scatter(lax.dot_general(block, paired, contract, preferred_eleme...  310 us
    all_gather x2, waiting for transfers between devices, all_blocks(): tiles = lax.all_gather(tiles, axes[k])  125 us
    psum x5, blocking collectives, one_axis_at_a_time(): return functools.reduce(lax.psum, axes, x)  84.5 us
  transfers between devices with their start and end apart: 3, of which 3 were waited for; matrix products, arithmetic and copies ran while one was open for 0% of the time, Pallas kernels for 0%

commit v1 on v0

v1 whole, which is shorter than its diff:
```python
import math

import jax
import jax.numpy as jnp
from jax import lax
from jax.experimental import pallas as pl
from jax.experimental.pallas import tpu as pltpu
from jax.sharding import Mesh
from jax.sharding import PartitionSpec as P

DP = ("x", "y_lo", "z")
XZ = ("x", "z")
YZ = ("y_lo", "z")
SECTION = ("y_hi", "core")
EVERY = SECTION + DP

NX, NY, NZ = 4, 2, 8

beta_one = 0.9
beta_two = 0.95
correct_one = 1.0 - 0.9**20
correct_two = 1.0 - 0.95**20
adam_eps = 1e-08
decay_rate = 0.1
learn_rate = 0.1


def gradient_kernel(slots_ref, tails_ref, acts_ref, out_ref, paired_ref):
    tail = tails_ref.shape[0] // slots_ref.shape[0]

    @pl.when((pl.program_id(0) == 0) & (pl.program_id(1) == 0))
    def _():
        def place(t, carry):
            src = pl.ds(pl.multiple_of(t * tail, tail), tail)
            dst = pl.ds(pl.multiple_of(slots_ref[t] * tail, tail), tail)
            paired_ref[dst, :] = tails_ref[src, :]
            return carry

        lax.fori_loop(0, slots_ref.shape[0], place, 0)

    product = lax.dot_general(
        paired_ref[...],
        acts_ref[...],
        (((0,), (0,)), ((), ())),
        preferred_element_type=jnp.float32,
    ).astype(out_ref.dtype)
    rows = out_ref.shape[-1]
    for k in range(out_ref.shape[1]):
        out_ref[0, k, 0] = product[:, k * rows : (k + 1) * rows]


def gradient_terms(slots, tails, acts):
    tokens, width = acts.shape
    cols = tails.shape[1]
    rows = width // (NX * NY * NZ)
    return pl.pallas_call(
        gradient_kernel,
        grid_spec=pltpu.PrefetchScalarGridSpec(
            num_scalar_prefetch=1,
            grid=(NX, NY),
            in_specs=[
                pl.BlockSpec((tokens, cols), lambda i, j, s: (0, 0)),
                pl.BlockSpec((tokens, NZ * rows), lambda i, j, s: (0, i * NY + j)),
            ],
            out_specs=pl.BlockSpec((1, NZ, 1, cols, rows), lambda i, j, s: (i, 0, j, 0, 0)),
            scratch_shapes=[pltpu.VMEM((tokens, cols), tails.dtype)],
        ),
        out_shape=jax.ShapeDtypeStruct((NX, NZ, NY, cols, rows), jnp.bfloat16),
        name="gradient_terms",
    )(slots, tails, acts)


def swap_pair(x):
    return lax.ppermute(x, "y_lo", [(0, 1), (1, 0)])


def local(
    activations, tail_grads, tail_slots, master, moment1, moment2, overflow, clip_on, next_inputs
):
    acts = activations[0]
    tails = tail_grads[0]
    tok_dev, width = acts.shape
    cols = tails.shape[1]
    rows = master.shape[1]
    toks = next_inputs.shape[1]
    own = lax.axis_index("y_lo")

    tokens = next_inputs[0].reshape(toks, NX, NY * NZ, rows)
    tokens = tokens.transpose(2, 0, 1, 3)
    tokens = lax.all_to_all(tokens, YZ, 0, 0, tiled=True)

    terms = gradient_terms(tail_slots[0, 0], tails, acts)
    summed = lax.psum_scatter(
        terms.reshape(NX * NZ * NY * cols, rows), XZ, scatter_dimension=0, tiled=True
    ).reshape(NY, cols, rows)
    mine = lax.dynamic_index_in_dim(summed, own, 0, keepdims=False)
    theirs = lax.dynamic_index_in_dim(summed, 1 - own, 0, keepdims=False)
    total = mine.astype(jnp.float32) + swap_pair(theirs).astype(jnp.float32)
    gradient = total.T * (1.0 / (tok_dev * NX * NY * NZ))

    keep = (overflow[0, 0] == 0).astype(jnp.float32)
    sumsq = lax.psum(keep * jnp.sum(gradient * gradient), EVERY)
    norm_value = jnp.sqrt(sumsq)
    factor = jnp.where(clip_on[0] == 1, 1.0 / jnp.maximum(norm_value, 1.0), 1.0)
    clipped = gradient * factor
    old_master = master[0]
    m_next = beta_one * moment1[0] + (1.0 - beta_one) * clipped
    v_next = beta_two * moment2[0] + (1.0 - beta_two) * (clipped * clipped)
    update = (
        m_next / correct_one / (jnp.sqrt(v_next / correct_two) + adam_eps) + decay_rate * old_master
    )
    updated = jnp.where(keep > 0.5, old_master - learn_rate * update, old_master)
    weights = updated.astype(jnp.bfloat16)

    along_x = lax.all_gather(weights, "x")
    partial = jnp.einsum(
        "gtxr,xrc->gtc", tokens, along_x, preferred_element_type=jnp.float32
    ).astype(jnp.bfloat16)
    parts = lax.all_to_all(partial, YZ, 0, 0, tiled=True)
    result = jnp.sum(parts.astype(jnp.float32), axis=0)
    next_out = (result * (1.0 / math.sqrt(width))).astype(jnp.bfloat16)
    return (updated[None], next_out[None])


def solution(mesh):
    finer = Mesh(mesh.devices.reshape(2, 2, NX, NY, NZ), EVERY)
    return jax.shard_map(
        local,
        mesh=finer,
        in_specs=(
            P(SECTION, DP, None),
            P(SECTION, DP, None),
            P(SECTION, DP, None),
            P(SECTION, DP, None),
            P(SECTION, DP, None),
            P(SECTION, DP, None),
            P(SECTION, DP),
            P(SECTION),
            P(SECTION, DP, None),
        ),
        out_specs=(P(SECTION, DP, None), P(SECTION, DP, None)),
        check_vma=False,
    )
```

time: 571 us -> 380 us (0.67)
  waiting for transfers between devices: 435 us -> 234 us
  starting transfers between devices: 0.12 us -> 16.4 us
  matrix products: 17.1 us -> 1.22 us
  Pallas kernels: 0 us -> 9.86 us
  local copies, waits for them, and re-layouts: 9.7 us -> 3.65 us
    all_gather x2 -> x0, waiting for transfers between devices: 125 us -> none  [all_blocks(): tiles = lax.all_gather(tiles, axes[k])]
    reduce_scatter x1, waiting for transfers between devices: 310 us -> 222 us  [local(): lax.psum_scatter(terms.reshape(NX * NZ * NY * cols, rows), XZ, scatter_di...]
    dot_general x3 -> x1, matrix products: 17.1 us -> 1.22 us  [local(): jnp.einsum('gtxr,xrc->gtc', tokens, along_x, preferred_element_type=jnp.f...]
    all_to_all x0 -> x2, starting transfers between devices: none -> 15 us  [the longest x1 10.1 us: local(): tokens = lax.all_to_all(tokens, YZ, 0, 0, tiled=True)]
    all_to_all x0 -> x2, waiting for transfers between devices: none -> 11 us  [the longest x1 11 us: local(): parts = lax.all_to_all(partial, YZ, 0, 0, tiled=True)]
    pallas_call x0 -> x1, Pallas kernels: none -> 9.86 us  [gradient_terms(): pl.pallas_call(gradient_kernel, grid_spec=pltpu.PrefetchScalarGridSpec(nu...]
    transpose x1 -> x0, local copies, waits for them, and re-layouts: 7.58 us -> none  [all_blocks(): tiles = tiles.transpose(*back, *range(len(axes), tiles.ndim))]
    all_gather x1, blocking collectives: 4.51 us -> 11.8 us  [local(): along_x = lax.all_gather(weights, 'x')]
  transfers between devices with their start and end apart: 3 -> 4, of which waited for: 3 -> 3; matrix products, arithmetic and copies ran while one was open for 0% -> 2% of each run, Pallas kernels for 0% -> 0%
where the time goes in v1:
time: 380 us; the launch traced here: 377 us
  waiting for transfers between devices  234 us (62%)
  blocking collectives  91.5 us (24%)
  between operations  16.8 us (4%)
  starting transfers between devices  16.4 us (4%)
  Pallas kernels  9.86 us (3%)
    reduce_scatter x1, waiting for transfers between devices, local(): lax.psum_scatter(terms.reshape(NX * NZ * NY * cols, rows), XZ, scatter_di...  222 us
    psum x1, blocking collectives, local(): sumsq = lax.psum(keep * jnp.sum(gradient * gradient), EVERY)  79.6 us
    all_gather x1, blocking collectives, local(): along_x = lax.all_gather(weights, 'x')  11.8 us
    all_to_all x1, waiting for transfers between devices, local(): parts = lax.all_to_all(partial, YZ, 0, 0, tiled=True)  11 us
    all_to_all x1, starting transfers between devices, local(): tokens = lax.all_to_all(tokens, YZ, 0, 0, tiled=True)  10.1 us
    pallas_call x1, Pallas kernels, gradient_terms(): pl.pallas_call(gradient_kernel, grid_spec=pltpu.PrefetchScalarGridSpec(nu...  9.86 us
  transfers between devices with their start and end apart: 4, of which 3 were waited for; matrix products, arithmetic and copies ran while one was open for 2% of the time, Pallas kernels for 0%

profile of v1, /device:TPU:1, one launch (start us, length us, event | category | flops | bytes accessed | tf_op | source)
XLA Modules:
  0.0 376.6 jit_solution(13898999094260465993)
XLA Ops:
  7.2 0.0 reduce-scatter.2.cloned.1.call-start
  7.2 9.9 %gradient_terms.1 = bf16[4,8,2,512,128]{4,3,2,1,0:T(8,128)(2,1)} custom-call(s32[4]{0:T(128)} %bitcast.84, bf16[256,512]{1,0:T(8,128)(2,1)} %bitcast.83, bf16[256,8192]{1,0:T(8,128)(2,1)} %bitcast.75), custom_call_target="tpu_custom_call" | custom-call | tf_op jit(solution)/shard_map/gradient_terms/pallas_call | solution.py:56
  17.1 0.0 reduce-scatter.2.cloned.1.call-update
  17.1 0.1 copy.18
  17.2 1.2 copy.20
  18.4 10.1 %all-to-all-start = ((bf16[16,32,4,128]{3,1,2,0:T(8,128)(2,1)}), bf16[16,32,4,128]{3,1,2,0:T(8,128)(2,1)S(1)}, u32[]{:S(2)}, u32[]{:S(2)}) async-start(bf16[16,32,4,128]{3,1,2,0:T(8,128)(2,1)} %bitcast.73), calls=%async_computation.1 | async-start | bytes 1048576 | tf_op jit(solution)/shard_map/all_to_all | solution.py:90
  28.6 221.8 %reduce-scatter.2.cloned.1.call-done = bf16[1024,128]{1,0:T(8,128)(2,1)} async-done(((bf16[32768,128]{1,0:T(8,128)(2,1)}), bf16[1024,128]{1,0:T(8,128)(2,1)}) %reduce-scatter.2.cloned.1.call-update) | async-done | bytes 262160 | tf_op jit(solution)/shard_map/reduce_scatter | solution.py:93
  250.4 0.9 dynamic-slice_bitcast_fusion
  251.3 1.3 collective-permute-start
  253.9 0.1 copy.11
  254.1 0.1 copy.12
  254.2 0.1 copy.13
  254.3 0.9 collective-permute-done
  255.2 1.6 multiply_reduce_fusion
  257.5 79.6 %psum.7 = f32[]{:T(128)} all-reduce(f32[]{:T(128)S(6)} %mul.86), channel_id=1, replica_groups=mesh['y_hi'=2,'core'=2,'x'=4,'y_lo'=2,'z'=8] {'y_hi','core','x','y_lo','z'}, use_global_device_ids=true, to_apply=%region_2.3 | all-reduce | flops 1 | bytes 8 | tf_op jit(solution)/shard_map/psum | solution.py:102
  337.8 1.2 fusion.10
  339.0 11.8 %all-gather = bf16[512,512]{0,1:T(8,128)(2,1)S(1)} all-gather(bf16[128,512]{0,1:T(8,128)(2,1)S(1)} %get-tuple-element.4), channel_id=2, replica_groups=mesh['y_hi'=2,'core'=2,'x'=4,'y_lo'=2,'z'=8] {'x'}, dimensions={0}, use_global_device_ids=true | all-gather | bytes 655360 | tf_op jit(solution)/shard_map/all_gather | solution.py:115
  350.8 0.2 copy.14
  351.1 1.2 fusion.1
  352.3 4.9 %all-to-all-start.1 = ((bf16[16,32,512]{2,1,0:T(8,128)(2,1)}), bf16[16,32,512]{2,1,0:T(8,128)(2,1)S(1)}, u32[]{:S(2)}, u32[]{:S(2)}) async-start(bf16[16,32,512]{2,1,0:T(8,128)(2,1)} %fusion.1), calls=%async_computation.2 | async-start | bytes 1048576 | tf_op jit(solution)/shard_map/all_to_all | solution.py:119
  357.2 0.8 copy.16
  358.0 11.0 %all-to-all-done.1 = bf16[16,32,512]{2,1,0:T(8,128)(2,1)S(1)} async-done(((bf16[16,32,512]{2,1,0:T(8,128)(2,1)}), bf16[16,32,512]{2,1,0:T(8,128)(2,1)S(1)}, u32[]{:S(2)}, u32[]{:S(2)}) %all-to-all-start.1) | async-done | bytes 524320 | tf_op jit(solution)/shard_map/all_to_all | solution.py:119
  369.0 0.1 convert_reduce_fusion
  369.1 0.6 fusion.9
  (9 shorter events, 0.0 us)
Async XLA Ops:
  7.2 243.2 %reduce-scatter.2.cloned.1.call-start = ((), (), s32[]{:S(2)}) async-start(), calls=%async_computation.3 | async-start | bytes 8650752 | tf_op jit(solution)/shard_map/reduce_scatter | solution.py:93
  7.2 9.9 %copy-start = (bf16[1,32,8192]{2,1,0:T(8,128)(2,1)S(1)}, bf16[1,32,8192]{2,1,0:T(8,128)(2,1)}, u32[]{:S(2)}) copy-start(bf16[1,32,8192]{2,1,0:T(8,128)(2,1)} %param.17) | copy-start | bytes 1572868
  17.1 236.8 %copy-start.1 = (f32[1,128,512]{2,1,0:T(8,128)S(1)}, f32[1,128,512]{2,1,0:T(8,128)}, u32[]{:S(2)}) copy-start(f32[1,128,512]{2,1,0:T(8,128)} %param.12) | copy-start | bytes 786436
  17.1 237.0 %copy-start.2 = (f32[1,128,512]{2,1,0:T(8,128)S(1)}, f32[1,128,512]{2,1,0:T(8,128)}, u32[]{:S(2)}) copy-start(f32[1,128,512]{2,1,0:T(8,128)} %param.13) | copy-start | bytes 786436
  17.1 237.1 %copy-start.3 = (f32[1,128,512]{2,1,0:T(8,128)S(1)}, f32[1,128,512]{2,1,0:T(8,128)}, u32[]{:S(2)}) copy-start(f32[1,128,512]{2,1,0:T(8,128)} %param.14) | copy-start | bytes 786436
  18.4 332.6 %all-to-all-start = ((bf16[16,32,4,128]{3,1,2,0:T(8,128)(2,1)}), bf16[16,32,4,128]{3,1,2,0:T(8,128)(2,1)S(1)}, u32[]{:S(2)}, u32[]{:S(2)}) async-start(bf16[16,32,4,128]{3,1,2,0:T(8,128)(2,1)} %bitcast.73), calls=%async_computation.1 | async-start | bytes 1048576 | tf_op jit(solution)/shard_map/all_to_all | solution.py:90
  251.3 3.9 %collective-permute-start = (bf16[512,128]{1,0:T(8,128)(2,1)S(1)}, bf16[512,128]{1,0:T(8,128)(2,1)S(1)}, u32[]{:S(2)}, u32[]{:S(2)}) collective-permute-start(bf16[512,128]{1,0:T(8,128)(2,1)S(1)} %dynamic-slice_bitcast_fusion), channel_id=1, source_target_pairs={{0,8},{8,0},{1,9},{9,1},{2,10},{10,2},{3,11},{11,3},{4,12},{12,4},... | collective-permute-start | bytes 393224 | tf_op jit(solution)/shard_map/ppermute | solution.py:74
  352.3 16.8 %all-to-all-start.1 = ((bf16[16,32,512]{2,1,0:T(8,128)(2,1)}), bf16[16,32,512]{2,1,0:T(8,128)(2,1)S(1)}, u32[]{:S(2)}, u32[]{:S(2)}) async-start(bf16[16,32,512]{2,1,0:T(8,128)(2,1)} %fusion.1), calls=%async_computation.2 | async-start | bytes 1048576 | tf_op jit(solution)/shard_map/all_to_all | solution.py:119
Sparse Core Ops, SparseCore 0:
  17.2 233.1 reduce-scatter.1

commit v2 on v1

v2 whole, which is shorter than its diff:
```python
import functools
import math

import jax
import jax.numpy as jnp
from jax import lax
from jax.experimental import pallas as pl
from jax.experimental.pallas import tpu as pltpu
from jax.sharding import Mesh
from jax.sharding import PartitionSpec as P

DP = ("x", "y_lo", "z")
YZ = ("y_lo", "z")
SECTION = ("y_hi", "core")
EVERY = SECTION + DP

NX, NY, NZ = 4, 2, 8


beta_one = 0.9
beta_two = 0.95
correct_one = 1.0 - 0.9**20
correct_two = 1.0 - 0.95**20
adam_eps = 1e-08
decay_rate = 0.1
learn_rate = 0.1

f32 = jnp.float32
bf16 = jnp.bfloat16

ROWS = 128
X_COLS, Z_COLS = 192, 320
X_HALF, Z_HALF = X_COLS // 2, Z_COLS // 2
Z_WIDE = NX * ROWS


def column(x, y, z):
    return pl.multiple_of((x * (NY * NZ) + y * NZ + z) * ROWS, ROWS)


def x_terms(where, away, pairs, acts):
    owner = lax.rem(where[0] + away, NX)
    step = 4
    for b in range(0, NY * NZ, step):
        part = acts[:, pl.ds(column(owner, 0, b), step * ROWS)]
        term = jnp.dot(pairs, part, preferred_element_type=f32)
        for k in range(step):
            yield b + k, term[:, k * ROWS : (k + 1) * ROWS]


def side_columns(where, side, away, acts, turn=0):
    owner = lax.rem(where[1] + away, NZ)
    xs = [lax.rem(turn + k, NX) for k in range(NX)]
    return jnp.concatenate([acts[:, pl.ds(column(x, side, owner), ROWS)] for x in xs], axis=1)


def partner_pairs(joined):
    tail = joined[joined.shape[1] // 2 :, :]
    half = tail.shape[1] // 2
    return jnp.concatenate([tail[:, :half], tail[:, half:]], axis=0)


def z_terms(where, away, pairs, acts, joined, part):
    own = jnp.dot(
        pairs[...], side_columns(where, where[2], away, acts), preferred_element_type=f32
    )
    term = own + jnp.dot(partner_pairs(joined), part, preferred_element_type=f32)
    for k in range(NX):
        yield k, term[:, k * ROWS : (k + 1) * ROWS]


def first_kernel(where, slots, tails, acts, x_pairs, z_pairs, xp, xm, *refs):
    gives, placed = refs[:-1], refs[-1]
    tail = tails.shape[0] // slots.shape[0]

    def place(t, carry):
        src = pl.ds(pl.multiple_of(t * tail, tail), tail)
        dst = pl.ds(pl.multiple_of(slots[t] * tail, tail), tail)
        placed[dst, :] = tails[src, :]
        return carry

    lax.fori_loop(0, slots.shape[0], place, 0)
    pairs = placed[...].astype(f32).T.astype(bf16)
    x_pairs[...] = pairs[:X_COLS]
    z_pairs[...] = pairs[X_COLS:]
    tokens = acts.shape[0]
    for k, give in enumerate(gives):
        away = NZ // 2 - k
        for n, far in enumerate((away,) if away in (0, NZ // 2) else (away, NZ - away)):
            give[:tokens, n * Z_WIDE : (n + 1) * Z_WIDE] = side_columns(
                where, 1 - where[2], far, acts
            )
    gives[0][tokens:, :tokens] = pairs[X_COLS : X_COLS + Z_HALF]
    gives[0][tokens:, tokens:] = pairs[X_COLS + Z_HALF :]
    for b, term in x_terms(where, NX // 2, pairs[:X_COLS], acts):
        xp[b] = term[:X_HALF].astype(bf16)
        xm[b] = term[X_HALF:].astype(bf16)


def second_x_kernel(where, pairs, acts, got_p, got_m, out_p, out_m):
    for b, term in x_terms(where, 1, pairs[...], acts):
        out_p[b, :X_HALF] = (term[:X_HALF] + got_p[b].astype(f32)).astype(bf16)
        out_p[b, X_HALF:] = term[X_HALF:].astype(bf16)
    for b, term in x_terms(where, NX - 1, pairs[...], acts):
        out_m[b, :X_HALF] = term[:X_HALF].astype(bf16)
        out_m[b, X_HALF:] = (term[X_HALF:] + got_m[b].astype(f32)).astype(bf16)


def last_x_kernel(where, pairs, acts, got_p, got_m, out):
    for b, term in x_terms(where, 0, pairs[...], acts):
        out[b] = (term + got_p[b].astype(f32) + got_m[b].astype(f32)).astype(bf16)


def first_z_kernel(where, pairs, acts, joined, out_p, out_m):
    part = joined[: acts.shape[0], :]
    for k, term in z_terms(where, NZ // 2, pairs, acts, joined, part):
        out_p[k] = term[:Z_HALF].astype(bf16)
        out_m[k] = term[Z_HALF:].astype(bf16)


def later_z_kernel(s, where, pairs, acts, joined, part, got_p, got_m, out_p, out_m):
    away = NZ // 2 - s
    for k, term in z_terms(where, away, pairs, acts, joined, part[:, :Z_WIDE]):
        if s == 1:
            out_p[k, :Z_HALF] = (term[:Z_HALF] + got_p[k].astype(f32)).astype(bf16)
            out_p[k, Z_HALF:] = term[Z_HALF:].astype(bf16)
        else:
            out_p[k] = (term + got_p[k].astype(f32)).astype(bf16)
    for k, term in z_terms(where, NZ - away, pairs, acts, joined, part[:, Z_WIDE:]):
        if s == 1:
            out_m[k, :Z_HALF] = term[:Z_HALF].astype(bf16)
            out_m[k, Z_HALF:] = (term[Z_HALF:] + got_m[k].astype(f32)).astype(bf16)
        else:
            out_m[k] = (term + got_m[k].astype(f32)).astype(bf16)


def last_z_kernel(where, pairs, acts, joined, part, got_p, got_m, own, *sends):
    mine = jnp.dot(
        pairs[...], side_columns(where, where[2], 0, acts, where[0]), preferred_element_type=f32
    )
    xs = [lax.rem(where[0] + r, NX) for r in range(NX)]
    parts = [part[:, pl.ds(pl.multiple_of(x * ROWS, ROWS), ROWS)] for x in xs]
    term = mine + jnp.dot(
        partner_pairs(joined), jnp.concatenate(parts, axis=1), preferred_element_type=f32
    )
    for r, x in enumerate(xs):
        total = term[:, r * ROWS : (r + 1) * ROWS] + got_p[x].astype(f32) + got_m[x].astype(f32)
        if r == 0:
            own[...] = total
        else:
            sends[r - 1][...] = total.astype(bf16)


def gradient_kernel(scale, overflow, on_x, own, *refs):
    gots, (grad, squares) = refs[: NX - 1], refs[NX - 1 :]
    first = on_x[0].astype(f32)
    for k in range(1, on_x.shape[0]):
        first += on_x[k].astype(f32)
    second = own[...]
    for got in gots:
        second += got[...].astype(f32)
    total = jnp.concatenate([first, second], axis=0).T * scale
    grad[...] = total
    kept = jnp.where(overflow[0, 0] == 0, 1.0, 0.0)
    squares[...] = jnp.broadcast_to(jnp.sum(total * total) * kept, squares.shape)


def tokens_kernel(where, mine, out):
    for r in range(NX):
        owner = lax.rem(where[0] + r, NX)
        for g in range(NY * NZ):
            start = pl.multiple_of((owner * (NY * NZ) + g) * ROWS, ROWS)
            out[g, :, r * ROWS : (r + 1) * ROWS] = mine[:, pl.ds(start, ROWS)]


def near(x):
    return pltpu.with_memory_space_constraint(x, pltpu.VMEM)


SCALARS = pl.BlockSpec(memory_space=pltpu.SMEM)
GRANT = pltpu.CompilerParams(vmem_limit_bytes=8 * 2**20)
NEAR = pl.BlockSpec(memory_space=pltpu.VMEM)


def on_core(kernel, scalars, arrays, outs, scratch=()):
    return pl.pallas_call(
        kernel,
        in_specs=[SCALARS] * len(scalars) + [NEAR] * len(arrays),
        out_specs=[NEAR] * len(outs),
        out_shape=list(outs),
        scratch_shapes=scratch,
        compiler_params=GRANT,
    )(*scalars, *[near(a) for a in arrays])


def shift(x, axis, n, by):
    return lax.ppermute(x, axis, [(i, (i + by) % n) for i in range(n)])


def both(plus, minus, axis, n):
    return shift(plus, axis, n, 1), shift(minus, axis, n, -1)


def swap_side(x):
    return shift(x, "y_lo", NY, 1)


def sum_terms(where, slots, tails, acts):
    tokens = acts.shape[0]
    x_blocks = NY * NZ
    two = lambda *shape: [pltpu.VMEM(shape, bf16)] * 2
    wide = [Z_WIDE] + [2 * Z_WIDE] * (NZ // 2 - 1) + [Z_WIDE]
    tall = [tokens + Z_HALF] + [tokens] * (NZ // 2)
    outs = [pltpu.VMEM((X_COLS, tokens), bf16), pltpu.VMEM((Z_COLS, tokens), bf16)]
    outs += two(x_blocks, X_HALF, ROWS)
    outs += [pltpu.VMEM(shape, bf16) for shape in zip(tall, wide)]
    x_pairs, z_pairs, xp, xm, *gives = on_core(
        first_kernel, [where, slots], [tails, acts], outs, [pltpu.VMEM(tails.shape, bf16)]
    )

    gots = both(xp, xm, "x", NX)
    joined, *parts = [swap_side(give) for give in gives]

    sends = on_core(second_x_kernel, [where], [x_pairs, acts, *gots], two(x_blocks, X_COLS, ROWS))
    gots = both(*sends, "x", NX)
    (on_x,) = on_core(
        last_x_kernel,
        [where],
        [x_pairs, acts, *gots],
        [jax.ShapeDtypeStruct((x_blocks, X_COLS, ROWS), bf16)],
    )
    on_x = lax.all_to_all(on_x, YZ, 0, 0, tiled=True)

    sends = on_core(first_z_kernel, [where], [z_pairs, acts, joined], two(NX, Z_HALF, ROWS))
    gots = both(*sends, "z", NZ)
    for s in range(1, NZ // 2):
        sends = on_core(
            functools.partial(later_z_kernel, s),
            [where],
            [z_pairs, acts, joined, parts[s - 1], *gots],
            two(NX, Z_COLS, ROWS),
        )
        gots = both(*sends, "z", NZ)
    piece = lambda t: pltpu.VMEM((Z_COLS, ROWS), t)
    own, *sends = on_core(
        last_z_kernel,
        [where],
        [z_pairs, acts, joined, parts[-1], *gots],
        [piece(f32)] + [piece(bf16)] * (NX - 1),
    )
    gots = [shift(send, "x", NX, r + 1) for r, send in enumerate(sends)]
    return on_x, own, gots


def local(
    activations, tail_grads, tail_slots, master, moment1, moment2, overflow, clip_on, next_inputs
):
    acts = activations[0]
    tails = tail_grads[0]
    tok_dev, width = acts.shape
    toks = next_inputs.shape[1]
    where = jnp.stack([lax.axis_index(a) for a in ("x", "z", "y_lo")]).astype(jnp.int32)

    tokens = jax.ShapeDtypeStruct((NY * NZ, toks, NX * ROWS), bf16)
    (tokens,) = on_core(tokens_kernel, [where], [next_inputs[0]], [tokens])
    tokens = lax.all_to_all(tokens, YZ, 0, 0, tiled=True)

    on_x, own, gots = sum_terms(where, tail_slots[0, 0], tails, acts)
    gradient, part_sq = on_core(
        functools.partial(gradient_kernel, 1.0 / (tok_dev * NX * NY * NZ)),
        [overflow],
        [on_x, own, *gots],
        [pltpu.VMEM((ROWS, X_COLS + Z_COLS), f32), pltpu.VMEM((1, 128), f32)],
    )
    keep = (overflow[0, 0] == 0).astype(f32)
    part_sq = part_sq + shift(part_sq, "core", 2, 1)
    by_y = [lax.ppermute(part_sq, ("y_hi", "y_lo"), [(i, i ^ m) for i in range(4)]) for m in (1, 2, 3)]
    part_sq = (part_sq + by_y[0]) + (by_y[1] + by_y[2])
    part_sq = jnp.broadcast_to(part_sq[None], (NX * NZ, 1, 128))
    sumsq = jnp.sum(lax.all_to_all(part_sq, ("x", "z"), 0, 0, tiled=True), axis=0)[0, 0]
    norm_value = jnp.sqrt(sumsq)
    factor = jnp.where(clip_on[0] == 1, 1.0 / jnp.maximum(norm_value, 1.0), 1.0)
    clipped = gradient * factor
    old_master = master[0]
    m_next = beta_one * moment1[0] + (1.0 - beta_one) * clipped
    v_next = beta_two * moment2[0] + (1.0 - beta_two) * (clipped * clipped)
    update = (
        m_next / correct_one / (jnp.sqrt(v_next / correct_two) + adam_eps) + decay_rate * old_master
    )
    updated = jnp.where(keep > 0.5, old_master - learn_rate * update, old_master)
    weights = updated.astype(bf16)

    along_x = jnp.concatenate(
        [weights] + [shift(weights, "x", NX, -r) for r in range(1, NX)], axis=0
    )
    partial = jnp.einsum("gtk,kc->gtc", tokens, along_x, preferred_element_type=f32).astype(bf16)
    parts = lax.all_to_all(partial, YZ, 0, 0, tiled=True)
    result = jnp.sum(parts.astype(f32), axis=0)
    next_out = (result * (1.0 / math.sqrt(width))).astype(bf16)
    return (updated[None], next_out[None])


def solution(mesh):
    finer = Mesh(mesh.devices.reshape(2, 2, NX, NY, NZ), EVERY)
    return jax.shard_map(
        local,
        mesh=finer,
        in_specs=(
            P(SECTION, DP, None),
            P(SECTION, DP, None),
            P(SECTION, DP, None),
            P(SECTION, DP, None),
            P(SECTION, DP, None),
            P(SECTION, DP, None),
            P(SECTION, DP),
            P(SECTION),
            P(SECTION, DP, None),
        ),
        out_specs=(P(SECTION, DP, None), P(SECTION, DP, None)),
        check_vma=False,
    )
```

time: 380 us -> 179 us (0.47)
  the two profiles are of different devices: /device:TPU:1 before, /device:TPU:40 now
where the time goes in v2:
time: 179 us; the launch traced here: 178 us
  waiting for transfers between devices  82.1 us (46%)
  starting transfers between devices  54.6 us (31%)
  blocking collectives  18.3 us (10%)
  Pallas kernels  12.3 us (7%)
  local copies, waits for them, and re-layouts  6.63 us (4%)
  between operations  2.26 us (1%)
    ppermute x24, waiting for transfers between devices, shift(): return lax.ppermute(x, axis, [(i, (i + by) % n) for i in range(n)])  63.8 us
    ppermute x24, starting transfers between devices, shift(): return lax.ppermute(x, axis, [(i, (i + by) % n) for i in range(n)])  26.4 us
    all_to_all x1, blocking collectives, local(): parts = lax.all_to_all(partial, YZ, 0, 0, tiled=True)  18.3 us
    pallas_call x10, Pallas kernels, on_core(): pl.pallas_call(kernel, in_specs=[SCALARS] * len(scalars) + [NEAR] * len(a...  12.3 us
    all_to_all x1, starting transfers between devices, sum_terms(): on_x = lax.all_to_all(on_x, YZ, 0, 0, tiled=True)  9.49 us
    all_to_all x1, waiting for transfers between devices, local(): tokens = lax.all_to_all(tokens, YZ, 0, 0, tiled=True)  8.36 us
    all_to_all x1, starting transfers between devices, local(): tokens = lax.all_to_all(tokens, YZ, 0, 0, tiled=True)  7.75 us
    all_to_all x1, starting transfers between devices, local(): lax.all_to_all(part_sq, ('x', 'z'), 0, 0, tiled=True)  7.5 us
  transfers between devices with their start and end apart: 30, of which 19 were waited for; matrix products, arithmetic and copies ran while one was open for 1% of the time, Pallas kernels for 5%

profile of v2, /device:TPU:40, one launch (start us, length us, event | category | flops | bytes accessed | tf_op | source)
XLA Modules:
  0.0 178.3 jit_solution(16668898077473015658)
XLA Ops:
  0.7 2.2 %copy-done = bf16[1,256,8192]{2,1,0:T(8,128)(2,1)S(1)} copy-done((bf16[1,256,8192]{2,1,0:T(8,128)(2,1)S(1)}, bf16[1,256,8192]{2,1,0:T(8,128)(2,1)}, u32[]{:S(2)}) %copy-start) | copy-done | bytes 4194328
  4.5 2.3 %shard_map.104 = (bf16[192,256]{1,0:T(8,128)(2,1)S(1)}, bf16[320,256]{1,0:T(8,128)(2,1)S(1)}, bf16[16,96,128]{2,1,0:T(8,128)(2,1)S(1)}, bf16[16,96,128]{2,1,0:T(...) custom-call(s32[3]{0:T(128)S(1)} %pad_add_fusion.where, ...), custom_call_target="tpu_custom_call" | custom-call | tf_op jit(solution)/shard_map/pallas_call | solution.py:186
  10.0 8.8 %collective-permute-done.got_p = bf16[16,96,128]{2,1,0:T(8,128)(2,1)S(1)} collective-permute-done((bf16[16,96,128]{2,1,0:T(8,128)(2,1)S(1)}, bf16[16,96,128]{2,1,0:T(8,128)(2,1)S(1)}, u32[]{:S(2)}, u32[]{:S(2)}) %collective-permute-start) | collective-permute-done | bytes 393248 | tf_op jit(solution)/shard_map/ppermute | solution.py:197
  25.4 14.4 %collective-permute-done.2.got_p = bf16[16,192,128]{2,1,0:T(8,128)(2,1)S(1)} collective-permute-done((bf16[16,192,128]{2,1,0:T(8,128)(2,1)S(1)}, bf16[16,192,128]{2,1,0:T(8,128)(2,1)S(1)}, u32[]{:S(2)}, u32[]{:S(2)}) %collective-permute-start.2) | collective-permute-done | bytes 786464 | tf_op jit(solution)/shard_map/ppermute | solution.py:197
  39.8 1.9 %shard_map.106 = bf16[16,192,128]{2,1,0:T(8,128)(2,1)} custom-call(s32[3]{0:T(128)S(1)} %pad_add_fusion.where, bf16[192,256]{1,0:T(8,128)(2,1)S(1)} %get-tuple-element.27.pairs, bf16[256,8192]{1,0:T(8,128)(2,1)S(1)} %bitcast.54, bf16[16,192,128]{2,1,0:T(8,128)(2,1)S(1)} %collective-permute-done.2.got_p, bf16[16,192,128]{2,1,0:T(8,128)(2,1)S(1)} %collective-permute-done.3.got_m), custom_call_target="tpu_custom_call" | custom-call | tf_op jit(solution)/shard_map/pallas_call | solution.py:186
  41.7 9.5 %all-to-all-start = ((bf16[16,192,128]{2,1,0:T(8,128)(2,1)}), bf16[16,192,128]{2,1,0:T(8,128)(2,1)S(1)}, u32[]{:S(2)}, u32[]{:S(2)}) async-start(bf16[16,192,128]{2,1,0:T(8,128)(2,1)} %shard_map.106), calls=%async_computation | async-start | bytes 1572864 | tf_op jit(solution)/shard_map/all_to_all | solution.py:232
  51.7 2.2 %copy-done.2 = bf16[1,256,8192]{2,1,0:T(8,128)(2,1)S(1)} copy-done((bf16[1,256,8192]{2,1,0:T(8,128)(2,1)S(1)}, bf16[1,256,8192]{2,1,0:T(8,128)(2,1)}, u32[]{:S(2)}) %copy-start.2) | copy-done | bytes 4194328
  55.1 1.8 %collective-permute-start.9 = (bf16[4,160,128]{2,1,0:T(8,128)(2,1)S(1)}, bf16[4,160,128]{2,1,0:T(8,128)(2,1)S(1)}, u32[]{:S(2)}, u32[]{:S(2)}) collective-permute-start(bf16[4,160,128]{2,1,0:T(8,128)(2,1)S(1)} %get-tuple-element.38), channel_id=1, source_target_pairs={{0,1},{1,2},{2,3},{3,4},{4,5},{5,6},{6,7},{7,0},{8,9},{9,10},{10,1... | collective-permute-start | bytes 491528 | tf_op jit(solution)/shard_map/ppermute | solution.py:197
  56.9 14.7 %collective-permute-done.10.got_m = bf16[4,160,128]{2,1,0:T(8,128)(2,1)S(1)} collective-permute-done((bf16[4,160,128]{2,1,0:T(8,128)(2,1)S(1)}, bf16[4,160,128]{2,1,0:T(8,128)(2,1)S(1)}, u32[]{:S(2)}, u32[]{:S(2)}) %collective-permute-start.10) | collective-permute-done | bytes 163872 | tf_op jit(solution)/shard_map/ppermute | solution.py:197
  75.4 6.1 %collective-permute-done.11.got_p = bf16[4,320,128]{2,1,0:T(8,128)(2,1)S(1)} collective-permute-done((bf16[4,320,128]{2,1,0:T(8,128)(2,1)S(1)}, bf16[4,320,128]{2,1,0:T(8,128)(2,1)S(1)}, u32[]{:S(2)}, u32[]{:S(2)}) %collective-permute-start.11) | collective-permute-done | bytes 327712 | tf_op jit(solution)/shard_map/ppermute | solution.py:197
  81.5 2.0 %collective-permute-done.12.got_m = bf16[4,320,128]{2,1,0:T(8,128)(2,1)S(1)} collective-permute-done((bf16[4,320,128]{2,1,0:T(8,128)(2,1)S(1)}, bf16[4,320,128]{2,1,0:T(8,128)(2,1)S(1)}, u32[]{:S(2)}, u32[]{:S(2)}) %collective-permute-start.12) | collective-permute-done | bytes 327712 | tf_op jit(solution)/shard_map/ppermute | solution.py:197
  84.7 2.0 %collective-permute-start.13 = (bf16[4,320,128]{2,1,0:T(8,128)(2,1)S(1)}, bf16[4,320,128]{2,1,0:T(8,128)(2,1)S(1)}, u32[]{:S(2)}, u32[]{:S(2)}) collective-permute-start(bf16[4,320,128]{2,1,0:T(8,128)(2,1)S(1)} %get-tuple-element.42), channel_id=1, source_target_pairs={{0,1},{1,2},{2,3},{3,4},{4,5},{5,6},{6,7},{7,0},{8,9},{9,10},{10,1... | collective-permute-start | bytes 983048 | tf_op jit(solution)/shard_map/ppermute | solution.py:197
  87.2 5.6 %collective-permute-done.13.got_p = bf16[4,320,128]{2,1,0:T(8,128)(2,1)S(1)} collective-permute-done((bf16[4,320,128]{2,1,0:T(8,128)(2,1)S(1)}, bf16[4,320,128]{2,1,0:T(8,128)(2,1)S(1)}, u32[]{:S(2)}, u32[]{:S(2)}) %collective-permute-start.13) | collective-permute-done | bytes 327712 | tf_op jit(solution)/shard_map/ppermute | solution.py:197
  95.1 1.8 %collective-permute-start.15 = (bf16[4,320,128]{2,1,0:T(8,128)(2,1)S(1)}, bf16[4,320,128]{2,1,0:T(8,128)(2,1)S(1)}, u32[]{:S(2)}, u32[]{:S(2)}) collective-permute-start(bf16[4,320,128]{2,1,0:T(8,128)(2,1)S(1)} %get-tuple-element.44), channel_id=1, source_target_pairs={{0,1},{1,2},{2,3},{3,4},{4,5},{5,6},{6,7},{7,0},{8,9},{9,10},{10,1... | collective-permute-start | bytes 983048 | tf_op jit(solution)/shard_map/ppermute | solution.py:197
  97.9 5.8 %collective-permute-done.5.part = bf16[256,512]{1,0:T(8,128)(2,1)S(1)} collective-permute-done((bf16[256,512]{1,0:T(8,128)(2,1)S(1)}, bf16[256,512]{1,0:T(8,128)(2,1)S(1)}, u32[]{:S(2)}, u32[]{:S(2)}) %collective-permute-start.5) | collective-permute-done | bytes 262176 | tf_op jit(solution)/shard_map/ppermute | solution.py:197
  105.3 3.9 %collective-permute-start.18 = (bf16[320,128]{1,0:T(8,128)(2,1)S(1)}, bf16[320,128]{1,0:T(8,128)(2,1)S(1)}, u32[]{:S(2)}, u32[]{:S(2)}) collective-permute-start(bf16[320,128]{1,0:T(8,128)(2,1)S(1)} %get-tuple-element.48), channel_id=1, source_target_pairs={{0,32},{16,48},{32,0},{48,16},{1,33},{17,49},{33,1},{49,17},{2,34}... | collective-permute-start | bytes 245768 | tf_op jit(solution)/shard_map/ppermute | solution.py:197
  110.7 1.8 collective-permute-done.18.refs_1_
  115.7 2.3 %collective-permute-start.22 = (f32[1,128]{1,0:T(1,128)S(1)}, f32[1,128]{1,0:T(1,128)S(1)}, u32[]{:S(2)}, u32[]{:S(2)}) collective-permute-start(f32[1,128]{1,0:T(1,128)S(1)} %add.27), channel_id=1, source_target_pairs={{0,128},{8,136},{128,0},{136,8},{1,129},{9,137},{129,1},{137,9},{2... | collective-permute-start | bytes 1544 | tf_op jit(solution)/shard_map/ppermute | solution.py:277
  118.8 2.0 %collective-permute-done.22 = f32[1,128]{1,0:T(1,128)S(1)} collective-permute-done((f32[1,128]{1,0:T(1,128)S(1)}, f32[1,128]{1,0:T(1,128)S(1)}, u32[]{:S(2)}, u32[]{:S(2)}) %collective-permute-start.22) | collective-permute-done | bytes 544 | tf_op jit(solution)/shard_map/ppermute | solution.py:277
  122.2 7.5 %all-to-all-start.1 = ((f32[32,1,128]{2,1,0:T(1,128)}), f32[32,1,128]{2,1,0:T(1,128)S(1)}, u32[]{:S(2)}, u32[]{:S(2)}) async-start(f32[32,1,128]{2,1,0:T(1,128)} %broadcast_in_dim.13), calls=%async_computation.1 | async-start | bytes 32768 | tf_op jit(solution)/shard_map/all_to_all | solution.py:280
  131.2 7.1 %all-to-all-done.1 = f32[32,1,128]{2,1,0:T(1,128)S(1)} async-done(((f32[32,1,128]{2,1,0:T(1,128)}), f32[32,1,128]{2,1,0:T(1,128)S(1)}, u32[]{:S(2)}, u32[]{:S(2)}) %all-to-all-start.1) | async-done | bytes 16416 | tf_op jit(solution)/shard_map/all_to_all | solution.py:280
  138.3 7.8 %all-to-all-start.2 = ((bf16[16,32,512]{2,1,0:T(8,128)(2,1)}), bf16[16,32,512]{2,1,0:T(8,128)(2,1)S(1)}, u32[]{:S(2)}, u32[]{:S(2)}) async-start(bf16[16,32,512]{2,1,0:T(8,128)(2,1)} %shard_map.113), calls=%async_computation.2 | async-start | bytes 1048576 | tf_op jit(solution)/shard_map/all_to_all | solution.py:266
  150.5 8.4 %all-to-all-done.2 = bf16[16,32,512]{2,1,0:T(8,128)(2,1)S(1)} async-done(((bf16[16,32,512]{2,1,0:T(8,128)(2,1)}), bf16[16,32,512]{2,1,0:T(8,128)(2,1)S(1)}, u32[]{:S(2)}, u32[]{:S(2)}) %all-to-all-start.2) | async-done | bytes 524320 | tf_op jit(solution)/shard_map/all_to_all | solution.py:266
  159.3 18.3 %all_to_all.20 = bf16[16,32,512]{2,1,0:T(8,128)(2,1)S(1)} all-to-all(bf16[16,32,512]{2,1,0:T(8,128)(2,1)S(1)} %convolution_convert_fusion), channel_id=1, replica_groups=mesh['y_hi'=2,'core'=2,'x'=4,'y_lo'=2,'z'=8] {'y_lo','z'}, dimensions={0} | all-to-all | bytes 1048576 | tf_op jit(solution)/shard_map/all_to_all | solution.py:297
  (78 shorter events, 36.0 us)
Async XLA Ops:
  6.8 12.1 %collective-permute-start = (bf16[16,96,128]{2,1,0:T(8,128)(2,1)S(1)}, bf16[16,96,128]{2,1,0:T(8,128)(2,1)S(1)}, u32[]{:S(2)}, u32[]{:S(2)}) collective-permute-start(bf16[16,96,128]{2,1,0:T(8,128)(2,1)S(1)} %get-tuple-element.28), channel_id=1, source_target_pairs={{0,16},{16,32},{32,48},{48,0},{1,17},{17,33},{33,49},{49,1},{2,18}... | collective-permute-start | bytes 1179656 | tf_op jit(solution)/shard_map/ppermute | solution.py:197
  8.3 10.6 %collective-permute-start.1 = (bf16[16,96,128]{2,1,0:T(8,128)(2,1)S(1)}, bf16[16,96,128]{2,1,0:T(8,128)(2,1)S(1)}, u32[]{:S(2)}, u32[]{:S(2)}) collective-permute-start(bf16[16,96,128]{2,1,0:T(8,128)(2,1)S(1)} %get-tuple-element.29), channel_id=1, source_target_pairs={{0,48},{16,0},{32,16},{48,32},{1,49},{17,1},{33,17},{49,33},{2,50}... | collective-permute-start | bytes 1179656 | tf_op jit(solution)/shard_map/ppermute | solution.py:197
  20.0 19.7 %collective-permute-start.2 = (bf16[16,192,128]{2,1,0:T(8,128)(2,1)S(1)}, bf16[16,192,128]{2,1,0:T(8,128)(2,1)S(1)}, u32[]{:S(2)}, u32[]{:S(2)}) collective-permute-start(bf16[16,192,128]{2,1,0:T(8,128)(2,1)S(1)} %get-tuple-element.30), channel_id=1, source_target_pairs={{0,16},{16,32},{32,48},{48,0},{1,17},{17,33},{33,49},{49,1},{2,18}... | collective-permute-start | bytes 2359304 | tf_op jit(solution)/shard_map/ppermute | solution.py:197
  21.6 18.2 %collective-permute-start.3 = (bf16[16,192,128]{2,1,0:T(8,128)(2,1)S(1)}, bf16[16,192,128]{2,1,0:T(8,128)(2,1)S(1)}, u32[]{:S(2)}, u32[]{:S(2)}) collective-permute-start(bf16[16,192,128]{2,1,0:T(8,128)(2,1)S(1)} %get-tuple-element.31), channel_id=1, source_target_pairs={{0,48},{16,0},{32,16},{48,32},{1,49},{17,1},{33,17},{49,33},{2,50}... | collective-permute-start | bytes 2359304 | tf_op jit(solution)/shard_map/ppermute | solution.py:197
  23.4 28.4 %collective-permute-start.4 = (bf16[416,512]{1,0:T(8,128)(2,1)S(1)}, bf16[416,512]{1,0:T(8,128)(2,1)S(1)}, u32[]{:S(2)}, u32[]{:S(2)}) collective-permute-start(bf16[416,512]{1,0:T(8,128)(2,1)S(1)} %get-tuple-element.33), channel_id=1, source_target_pairs={{0,8},{8,0},{1,9},{9,1},{2,10},{10,2},{3,11},{11,3},{4,12},{12,4},... | collective-permute-start | bytes 1277960 | tf_op jit(solution)/shard_map/ppermute | solution.py:197
  23.8 33.1 %collective-permute-start.8 = (bf16[256,1024]{1,0:T(8,128)(2,1)}, bf16[256,1024]{1,0:T(8,128)(2,1)S(1)}, u32[]{:S(2)}, u32[]{:S(2)}) collective-permute-start(bf16[256,1024]{1,0:T(8,128)(2,1)} %get-tuple-element.37), channel_id=1, source_target_pairs={{0,8},{8,0},{1,9},{9,1},{2,10},{10,2},{3,11},{11,3},{4,12},{12,4},... | collective-permute-start | bytes 1572872 | tf_op jit(solution)/shard_map/ppermute | solution.py:197
  41.7 72.0 %all-to-all-start = ((bf16[16,192,128]{2,1,0:T(8,128)(2,1)}), bf16[16,192,128]{2,1,0:T(8,128)(2,1)S(1)}, u32[]{:S(2)}, u32[]{:S(2)}) async-start(bf16[16,192,128]{2,1,0:T(8,128)(2,1)} %shard_map.106), calls=%async_computation | async-start | bytes 1572864 | tf_op jit(solution)/shard_map/all_to_all | solution.py:232
  51.2 24.2 %collective-permute-start.7 = (bf16[256,1024]{1,0:T(8,128)(2,1)S(1)}, bf16[256,1024]{1,0:T(8,128)(2,1)S(1)}, u32[]{:S(2)}, u32[]{:S(2)}) collective-permute-start(bf16[256,1024]{1,0:T(8,128)(2,1)S(1)} %get-tuple-element.36), channel_id=1, source_target_pairs={{0,8},{8,0},{1,9},{9,1},{2,10},{10,2},{3,11},{11,3},{4,12},{12,4},... | collective-permute-start | bytes 1572872 | tf_op jit(solution)/shard_map/ppermute | solution.py:197
  54.8 16.8 %collective-permute-start.10 = (bf16[4,160,128]{2,1,0:T(8,128)(2,1)S(1)}, bf16[4,160,128]{2,1,0:T(8,128)(2,1)S(1)}, u32[]{:S(2)}, u32[]{:S(2)}) collective-permute-start(bf16[4,160,128]{2,1,0:T(8,128)(2,1)S(1)} %get-tuple-element.39), channel_id=1, source_target_pairs={{0,7},{1,0},{2,1},{3,2},{4,3},{5,4},{6,5},{7,6},{8,15},{9,8},{10,9... | collective-permute-start | bytes 491528 | tf_op jit(solution)/shard_map/ppermute | solution.py:197
  55.1 16.6 %collective-permute-start.9 = (bf16[4,160,128]{2,1,0:T(8,128)(2,1)S(1)}, bf16[4,160,128]{2,1,0:T(8,128)(2,1)S(1)}, u32[]{:S(2)}, u32[]{:S(2)}) collective-permute-start(bf16[4,160,128]{2,1,0:T(8,128)(2,1)S(1)} %get-tuple-element.38), channel_id=1, source_target_pairs={{0,1},{1,2},{2,3},{3,4},{4,5},{5,6},{6,7},{7,0},{8,9},{9,10},{10,1... | collective-permute-start | bytes 491528 | tf_op jit(solution)/shard_map/ppermute | solution.py:197
  72.7 8.8 %collective-permute-start.11 = (bf16[4,320,128]{2,1,0:T(8,128)(2,1)S(1)}, bf16[4,320,128]{2,1,0:T(8,128)(2,1)S(1)}, u32[]{:S(2)}, u32[]{:S(2)}) collective-permute-start(bf16[4,320,128]{2,1,0:T(8,128)(2,1)S(1)} %get-tuple-element.40), channel_id=1, source_target_pairs={{0,1},{1,2},{2,3},{3,4},{4,5},{5,6},{6,7},{7,0},{8,9},{9,10},{10,1... | collective-permute-start | bytes 983048 | tf_op jit(solution)/shard_map/ppermute | solution.py:197
  74.3 9.3 %collective-permute-start.12 = (bf16[4,320,128]{2,1,0:T(8,128)(2,1)S(1)}, bf16[4,320,128]{2,1,0:T(8,128)(2,1)S(1)}, u32[]{:S(2)}, u32[]{:S(2)}) collective-permute-start(bf16[4,320,128]{2,1,0:T(8,128)(2,1)S(1)} %get-tuple-element.41), channel_id=1, source_target_pairs={{0,7},{1,0},{2,1},{3,2},{4,3},{5,4},{6,5},{7,6},{8,15},{9,8},{10,9... | collective-permute-start | bytes 983048 | tf_op jit(solution)/shard_map/ppermute | solution.py:197
  74.8 12.4 %collective-permute-start.6 = (bf16[256,1024]{1,0:T(8,128)(2,1)S(1)}, bf16[256,1024]{1,0:T(8,128)(2,1)S(1)}, u32[]{:S(2)}, u32[]{:S(2)}) collective-permute-start(bf16[256,1024]{1,0:T(8,128)(2,1)S(1)} %get-tuple-element.35), channel_id=1, source_target_pairs={{0,8},{8,0},{1,9},{9,1},{2,10},{10,2},{3,11},{11,3},{4,12},{12,4},... | collective-permute-start | bytes 1572872 | tf_op jit(solution)/shard_map/ppermute | solution.py:197
  84.7 8.1 %collective-permute-start.13 = (bf16[4,320,128]{2,1,0:T(8,128)(2,1)S(1)}, bf16[4,320,128]{2,1,0:T(8,128)(2,1)S(1)}, u32[]{:S(2)}, u32[]{:S(2)}) collective-permute-start(bf16[4,320,128]{2,1,0:T(8,128)(2,1)S(1)} %get-tuple-element.42), channel_id=1, source_target_pairs={{0,1},{1,2},{2,3},{3,4},{4,5},{5,6},{6,7},{7,0},{8,9},{9,10},{10,1... | collective-permute-start | bytes 983048 | tf_op jit(solution)/shard_map/ppermute | solution.py:197
  86.7 7.3 %collective-permute-start.14 = (bf16[4,320,128]{2,1,0:T(8,128)(2,1)S(1)}, bf16[4,320,128]{2,1,0:T(8,128)(2,1)S(1)}, u32[]{:S(2)}, u32[]{:S(2)}) collective-permute-start(bf16[4,320,128]{2,1,0:T(8,128)(2,1)S(1)} %get-tuple-element.43), channel_id=1, source_target_pairs={{0,7},{1,0},{2,1},{3,2},{4,3},{5,4},{6,5},{7,6},{8,15},{9,8},{10,9... | collective-permute-start | bytes 983048 | tf_op jit(solution)/shard_map/ppermute | solution.py:197
  95.1 8.6 %collective-permute-start.15 = (bf16[4,320,128]{2,1,0:T(8,128)(2,1)S(1)}, bf16[4,320,128]{2,1,0:T(8,128)(2,1)S(1)}, u32[]{:S(2)}, u32[]{:S(2)}) collective-permute-start(bf16[4,320,128]{2,1,0:T(8,128)(2,1)S(1)} %get-tuple-element.44), channel_id=1, source_target_pairs={{0,1},{1,2},{2,3},{3,4},{4,5},{5,6},{6,7},{7,0},{8,9},{9,10},{10,1... | collective-permute-start | bytes 983048 | tf_op jit(solution)/shard_map/ppermute | solution.py:197
  97.0 7.1 %collective-permute-start.16 = (bf16[4,320,128]{2,1,0:T(8,128)(2,1)S(1)}, bf16[4,320,128]{2,1,0:T(8,128)(2,1)S(1)}, u32[]{:S(2)}, u32[]{:S(2)}) collective-permute-start(bf16[4,320,128]{2,1,0:T(8,128)(2,1)S(1)} %get-tuple-element.45), channel_id=1, source_target_pairs={{0,7},{1,0},{2,1},{3,2},{4,3},{5,4},{6,5},{7,6},{8,15},{9,8},{10,9... | collective-permute-start | bytes 983048 | tf_op jit(solution)/shard_map/ppermute | solution.py:197
  97.2 6.5 %collective-permute-start.5 = (bf16[256,512]{1,0:T(8,128)(2,1)S(1)}, bf16[256,512]{1,0:T(8,128)(2,1)S(1)}, u32[]{:S(2)}, u32[]{:S(2)}) collective-permute-start(bf16[256,512]{1,0:T(8,128)(2,1)S(1)} %copy-done.7), channel_id=1, source_target_pairs={{0,8},{8,0},{1,9},{9,1},{2,10},{10,2},{3,11},{11,3},{4,12},{12,4},... | collective-permute-start | bytes 786440 | tf_op jit(solution)/shard_map/ppermute | solution.py:197
  105.3 7.1 %collective-permute-start.18 = (bf16[320,128]{1,0:T(8,128)(2,1)S(1)}, bf16[320,128]{1,0:T(8,128)(2,1)S(1)}, u32[]{:S(2)}, u32[]{:S(2)}) collective-permute-start(bf16[320,128]{1,0:T(8,128)(2,1)S(1)} %get-tuple-element.48), channel_id=1, source_target_pairs={{0,32},{16,48},{32,0},{48,16},{1,33},{17,49},{33,1},{49,17},{2,34}... | collective-permute-start | bytes 245768 | tf_op jit(solution)/shard_map/ppermute | solution.py:197
  122.2 16.1 %all-to-all-start.1 = ((f32[32,1,128]{2,1,0:T(1,128)}), f32[32,1,128]{2,1,0:T(1,128)S(1)}, u32[]{:S(2)}, u32[]{:S(2)}) async-start(f32[32,1,128]{2,1,0:T(1,128)} %broadcast_in_dim.13), calls=%async_computation.1 | async-start | bytes 32768 | tf_op jit(solution)/shard_map/all_to_all | solution.py:280
  138.3 20.6 %all-to-all-start.2 = ((bf16[16,32,512]{2,1,0:T(8,128)(2,1)}), bf16[16,32,512]{2,1,0:T(8,128)(2,1)S(1)}, u32[]{:S(2)}, u32[]{:S(2)}) async-start(bf16[16,32,512]{2,1,0:T(8,128)(2,1)} %shard_map.113), calls=%async_computation.2 | async-start | bytes 1048576 | tf_op jit(solution)/shard_map/all_to_all | solution.py:266
  147.8 11.1 %collective-permute-start.24 = (bf16[128,512]{1,0:T(8,128)(2,1)S(1)}, bf16[128,512]{1,0:T(8,128)(2,1)S(1)}, u32[]{:S(2)}, u32[]{:S(2)}) collective-permute-start(bf16[128,512]{1,0:T(8,128)(2,1)S(1)} %get-tuple-element.52), channel_id=1, source_target_pairs={{0,48},{16,0},{32,16},{48,32},{1,49},{17,1},{33,17},{49,33},{2,50}... | collective-permute-start | bytes 393224 | tf_op jit(solution)/shard_map/ppermute | solution.py:197
  149.0 9.9 %collective-permute-start.25 = (bf16[128,512]{1,0:T(8,128)(2,1)S(1)}, bf16[128,512]{1,0:T(8,128)(2,1)S(1)}, u32[]{:S(2)}, u32[]{:S(2)}) collective-permute-start(bf16[128,512]{1,0:T(8,128)(2,1)S(1)} %get-tuple-element.52), channel_id=1, source_target_pairs={{0,32},{16,48},{32,0},{48,16},{1,33},{17,49},{33,1},{49,17},{2,34}... | collective-permute-start | bytes 393224 | tf_op jit(solution)/shard_map/ppermute | solution.py:197
  150.5 8.4 %collective-permute-start.26 = (bf16[128,512]{1,0:T(8,128)(2,1)S(1)}, bf16[128,512]{1,0:T(8,128)(2,1)S(1)}, u32[]{:S(2)}, u32[]{:S(2)}) collective-permute-start(bf16[128,512]{1,0:T(8,128)(2,1)S(1)} %get-tuple-element.52), channel_id=1, source_target_pairs={{0,16},{16,32},{32,48},{48,0},{1,17},{17,33},{33,49},{49,1},{2,18}... | collective-permute-start | bytes 393224 | tf_op jit(solution)/shard_map/ppermute | solution.py:197
  (17 other events, 273.1 us)

commit v3 on v2

--- a/solution.py
+++ b/solution.py
@@ -32,6 +32,7 @@
 X_COLS, Z_COLS = 192, 320
 X_HALF, Z_HALF = X_COLS // 2, Z_COLS // 2
 Z_WIDE = NX * ROWS
+EXTRA = 16
 
 
 def column(x, y, z):
@@ -134,16 +135,20 @@
             out_m[k] = (term + got_m[k].astype(f32)).astype(bf16)
 
 
-def last_z_kernel(where, pairs, acts, joined, part, got_p, got_m, own, *sends):
+def own_z_kernel(where, pairs, acts, joined, part, out):
     mine = jnp.dot(
         pairs[...], side_columns(where, where[2], 0, acts, where[0]), preferred_element_type=f32
     )
     xs = [lax.rem(where[0] + r, NX) for r in range(NX)]
     parts = [part[:, pl.ds(pl.multiple_of(x * ROWS, ROWS), ROWS)] for x in xs]
-    term = mine + jnp.dot(
+    out[...] = mine + jnp.dot(
         partner_pairs(joined), jnp.concatenate(parts, axis=1), preferred_element_type=f32
     )
-    for r, x in enumerate(xs):
+
+
+def last_z_kernel(where, term, got_p, got_m, own, *sends):
+    for r in range(NX):
+        x = lax.rem(where[0] + r, NX)
         total = term[:, r * ROWS : (r + 1) * ROWS] + got_p[x].astype(f32) + got_m[x].astype(f32)
         if r == 0:
             own[...] = total
@@ -170,7 +175,8 @@
         owner = lax.rem(where[0] + r, NX)
         for g in range(NY * NZ):
             start = pl.multiple_of((owner * (NY * NZ) + g) * ROWS, ROWS)
-            out[g, :, r * ROWS : (r + 1) * ROWS] = mine[:, pl.ds(start, ROWS)]
+            out[g, : mine.shape[0], r * ROWS : (r + 1) * ROWS] = mine[:, pl.ds(start, ROWS)]
+    out[:, mine.shape[0] :, :] = jnp.zeros((out.shape[0], EXTRA, out.shape[2]), out.dtype)
 
 
 def near(x):
@@ -242,11 +248,14 @@
         )
         gots = both(*sends, "z", NZ)
     piece = lambda t: pltpu.VMEM((Z_COLS, ROWS), t)
+    (term,) = on_core(
+        own_z_kernel,
+        [where],
+        [z_pairs, acts, joined, parts[-1]],
+        [pltpu.VMEM((Z_COLS, Z_WIDE), f32)],
+    )
     own, *sends = on_core(
-        last_z_kernel,
-        [where],
-        [z_pairs, acts, joined, parts[-1], *gots],
-        [piece(f32)] + [piece(bf16)] * (NX - 1),
+        last_z_kernel, [where], [term, *gots], [piece(f32)] + [piece(bf16)] * (NX - 1)
     )
     gots = [shift(send, "x", NX, r + 1) for r, send in enumerate(sends)]
     return on_x, own, gots
@@ -261,9 +270,8 @@
     toks = next_inputs.shape[1]
     where = jnp.stack([lax.axis_index(a) for a in ("x", "z", "y_lo")]).astype(jnp.int32)
 
-    tokens = jax.ShapeDtypeStruct((NY * NZ, toks, NX * ROWS), bf16)
+    tokens = jax.ShapeDtypeStruct((NY * NZ, toks + EXTRA, NX * ROWS), bf16)
     (tokens,) = on_core(tokens_kernel, [where], [next_inputs[0]], [tokens])
-    tokens = lax.all_to_all(tokens, YZ, 0, 0, tiled=True)
 
     on_x, own, gots = sum_terms(where, tail_slots[0, 0], tails, acts)
     gradient, part_sq = on_core(
@@ -273,11 +281,18 @@
         [pltpu.VMEM((ROWS, X_COLS + Z_COLS), f32), pltpu.VMEM((1, 128), f32)],
     )
     keep = (overflow[0, 0] == 0).astype(f32)
-    part_sq = part_sq + shift(part_sq, "core", 2, 1)
-    by_y = [lax.ppermute(part_sq, ("y_hi", "y_lo"), [(i, i ^ m) for i in range(4)]) for m in (1, 2, 3)]
-    part_sq = (part_sq + by_y[0]) + (by_y[1] + by_y[2])
-    part_sq = jnp.broadcast_to(part_sq[None], (NX * NZ, 1, 128))
-    sumsq = jnp.sum(lax.all_to_all(part_sq, ("x", "z"), 0, 0, tiled=True), axis=0)[0, 0]
+    others = ("y_hi", "core", "x")
+    part_sq = jnp.broadcast_to(part_sq[None], (4 * NX, 1, ROWS))
+    part_sq = jnp.sum(lax.all_to_all(part_sq, others, 0, 0, tiled=True), axis=0)[0, 0]
+    high = lax.reduce_precision(part_sq, 8, 7)
+    middle = lax.reduce_precision(part_sq - high, 8, 7)
+    pieces = jnp.stack([high, middle, part_sq - high - middle, 0.0 * high])
+    pieces = jnp.broadcast_to(jnp.repeat(pieces, ROWS)[None, None], (NY * NZ, EXTRA, NX * ROWS))
+    tokens = lax.dynamic_update_slice(tokens, pieces.astype(bf16), (0, toks, 0))
+    tokens = lax.all_to_all(tokens, YZ, 0, 0, tiled=True)
+    pieces = jnp.sum(tokens[:, toks, :].astype(f32), axis=0)
+    tokens = tokens[:, :toks]
+    sumsq = pieces[0] + pieces[ROWS] + pieces[2 * ROWS]
     norm_value = jnp.sqrt(sumsq)
     factor = jnp.where(clip_on[0] == 1, 1.0 / jnp.maximum(norm_value, 1.0), 1.0)
     clipped = gradient * factor

time: 179 us -> 197 us (1.10)
  the two profiles are of different devices: /device:TPU:40 before, /device:TPU:1 now
where the time goes in v3:
time: 197 us; the launch traced here: 194 us
  waiting for transfers between devices  85.6 us (43%)
  starting transfers between devices  55.4 us (28%)
  blocking collectives  21.6 us (11%)
  Pallas kernels  13 us (7%)
  between operations  8.53 us (4%)
  local copies, waits for them, and re-layouts  8.04 us (4%)
    ppermute x23, waiting for transfers between devices, shift(): return lax.ppermute(x, axis, [(i, (i + by) % n) for i in range(n)])  61.1 us
    ppermute x23, starting transfers between devices, shift(): return lax.ppermute(x, axis, [(i, (i + by) % n) for i in range(n)])  28.8 us
    all_to_all x1, blocking collectives, local(): parts = lax.all_to_all(partial, YZ, 0, 0, tiled=True)  21.6 us
    all_to_all x1, waiting for transfers between devices, local(): tokens = lax.all_to_all(tokens, YZ, 0, 0, tiled=True)  19.2 us
    pallas_call x11, Pallas kernels, on_core(): pl.pallas_call(kernel, in_specs=[SCALARS] * len(scalars) + [NEAR] * len(a...  13 us
    all_to_all x1, starting transfers between devices, local(): lax.all_to_all(part_sq, others, 0, 0, tiled=True)  11.8 us
    all_to_all x1, starting transfers between devices, sum_terms(): on_x = lax.all_to_all(on_x, YZ, 0, 0, tiled=True)  10.2 us
    unnamed x22, local copies, waits for them, and re-layouts  6.02 us
  transfers between devices with their start and end apart: 26, of which 18 were waited for; matrix products, arithmetic and copies ran while one was open for 0% of the time, Pallas kernels for 5%

profile of v3, /device:TPU:1, one launch (start us, length us, event | category | flops | bytes accessed | tf_op | source)
XLA Modules:
  0.0 194.4 jit_solution(14118643601721494474)
XLA Ops:
  0.7 2.2 %copy-done = bf16[1,256,8192]{2,1,0:T(8,128)(2,1)S(1)} copy-done((bf16[1,256,8192]{2,1,0:T(8,128)(2,1)S(1)}, bf16[1,256,8192]{2,1,0:T(8,128)(2,1)}, u32[]{:S(2)}) %copy-start) | copy-done | bytes 4194328
  4.5 2.3 %shard_map.104 = (bf16[192,256]{1,0:T(8,128)(2,1)S(1)}, bf16[320,256]{1,0:T(8,128)(2,1)S(1)}, bf16[16,96,128]{2,1,0:T(8,128)(2,1)S(1)}, bf16[16,96,128]{2,1,0:T(...) custom-call(s32[3]{0:T(128)S(1)} %pad_add_fusion.where, ...), custom_call_target="tpu_custom_call" | custom-call | tf_op jit(solution)/shard_map/pallas_call | solution.py:192
  6.8 2.0 %collective-permute-start = (bf16[16,96,128]{2,1,0:T(8,128)(2,1)S(1)}, bf16[16,96,128]{2,1,0:T(8,128)(2,1)S(1)}, u32[]{:S(2)}, u32[]{:S(2)}) collective-permute-start(bf16[16,96,128]{2,1,0:T(8,128)(2,1)S(1)} %get-tuple-element.28), channel_id=1, source_target_pairs={{0,16},{16,32},{32,48},{48,0},{1,17},{17,33},{33,49},{49,1},{2,18}... | collective-permute-start | bytes 1179656 | tf_op jit(solution)/shard_map/ppermute | solution.py:203
  10.1 6.6 %collective-permute-done.got_p = bf16[16,96,128]{2,1,0:T(8,128)(2,1)S(1)} collective-permute-done((bf16[16,96,128]{2,1,0:T(8,128)(2,1)S(1)}, bf16[16,96,128]{2,1,0:T(8,128)(2,1)S(1)}, u32[]{:S(2)}, u32[]{:S(2)}) %collective-permute-start) | collective-permute-done | bytes 393248 | tf_op jit(solution)/shard_map/ppermute | solution.py:203
  22.2 1.8 collective-permute-start.4
  24.1 13.8 %collective-permute-done.2.got_p = bf16[16,192,128]{2,1,0:T(8,128)(2,1)S(1)} collective-permute-done((bf16[16,192,128]{2,1,0:T(8,128)(2,1)S(1)}, bf16[16,192,128]{2,1,0:T(8,128)(2,1)S(1)}, u32[]{:S(2)}, u32[]{:S(2)}) %collective-permute-start.2) | collective-permute-done | bytes 786464 | tf_op jit(solution)/shard_map/ppermute | solution.py:203
  38.0 1.9 shard_map.106
  39.9 10.2 %all-to-all-start = ((bf16[16,192,128]{2,1,0:T(8,128)(2,1)}), bf16[16,192,128]{2,1,0:T(8,128)(2,1)S(1)}, u32[]{:S(2)}, u32[]{:S(2)}) async-start(bf16[16,192,128]{2,1,0:T(8,128)(2,1)} %shard_map.106), calls=%async_computation | async-start | bytes 1572864 | tf_op jit(solution)/shard_map/all_to_all | solution.py:238
  51.5 2.2 %copy-done.2 = bf16[1,256,8192]{2,1,0:T(8,128)(2,1)S(1)} copy-done((bf16[1,256,8192]{2,1,0:T(8,128)(2,1)S(1)}, bf16[1,256,8192]{2,1,0:T(8,128)(2,1)}, u32[]{:S(2)}) %copy-start.2) | copy-done | bytes 4194328
  54.6 2.5 %collective-permute-start.10 = (bf16[4,160,128]{2,1,0:T(8,128)(2,1)S(1)}, bf16[4,160,128]{2,1,0:T(8,128)(2,1)S(1)}, u32[]{:S(2)}, u32[]{:S(2)}) collective-permute-start(bf16[4,160,128]{2,1,0:T(8,128)(2,1)S(1)} %get-tuple-element.39), channel_id=1, source_target_pairs={{0,7},{1,0},{2,1},{3,2},{4,3},{5,4},{6,5},{7,6},{8,15},{9,8},{10,9... | collective-permute-start | bytes 491528 | tf_op jit(solution)/shard_map/ppermute | solution.py:203
  57.0 14.6 %collective-permute-done.10.got_m = bf16[4,160,128]{2,1,0:T(8,128)(2,1)S(1)} collective-permute-done((bf16[4,160,128]{2,1,0:T(8,128)(2,1)S(1)}, bf16[4,160,128]{2,1,0:T(8,128)(2,1)S(1)}, u32[]{:S(2)}, u32[]{:S(2)}) %collective-permute-start.10) | collective-permute-done | bytes 163872 | tf_op jit(solution)/shard_map/ppermute | solution.py:203
  74.7 2.2 %collective-permute-start.12 = (bf16[4,320,128]{2,1,0:T(8,128)(2,1)S(1)}, bf16[4,320,128]{2,1,0:T(8,128)(2,1)S(1)}, u32[]{:S(2)}, u32[]{:S(2)}) collective-permute-start(bf16[4,320,128]{2,1,0:T(8,128)(2,1)S(1)} %get-tuple-element.41), channel_id=1, source_target_pairs={{0,7},{1,0},{2,1},{3,2},{4,3},{5,4},{6,5},{7,6},{8,15},{9,8},{10,9... | collective-permute-start | bytes 983048 | tf_op jit(solution)/shard_map/ppermute | solution.py:203
  78.1 4.8 %collective-permute-done.11.got_p = bf16[4,320,128]{2,1,0:T(8,128)(2,1)S(1)} collective-permute-done((bf16[4,320,128]{2,1,0:T(8,128)(2,1)S(1)}, bf16[4,320,128]{2,1,0:T(8,128)(2,1)S(1)}, u32[]{:S(2)}, u32[]{:S(2)}) %collective-permute-start.11) | collective-permute-done | bytes 327712 | tf_op jit(solution)/shard_map/ppermute | solution.py:203
  84.0 2.0 %collective-permute-start.13 = (bf16[4,320,128]{2,1,0:T(8,128)(2,1)S(1)}, bf16[4,320,128]{2,1,0:T(8,128)(2,1)S(1)}, u32[]{:S(2)}, u32[]{:S(2)}) collective-permute-start(bf16[4,320,128]{2,1,0:T(8,128)(2,1)S(1)} %get-tuple-element.42), channel_id=1, source_target_pairs={{0,1},{1,2},{2,3},{3,4},{4,5},{5,6},{6,7},{7,0},{8,9},{9,10},{10,1... | collective-permute-start | bytes 983048 | tf_op jit(solution)/shard_map/ppermute | solution.py:203
  88.0 4.0 %collective-permute-done.13.got_p = bf16[4,320,128]{2,1,0:T(8,128)(2,1)S(1)} collective-permute-done((bf16[4,320,128]{2,1,0:T(8,128)(2,1)S(1)}, bf16[4,320,128]{2,1,0:T(8,128)(2,1)S(1)}, u32[]{:S(2)}, u32[]{:S(2)}) %collective-permute-start.13) | collective-permute-done | bytes 327712 | tf_op jit(solution)/shard_map/ppermute | solution.py:203
  94.8 1.8 collective-permute-start.16
  97.7 4.4 %collective-permute-done.5.part = bf16[256,512]{1,0:T(8,128)(2,1)S(1)} collective-permute-done((bf16[256,512]{1,0:T(8,128)(2,1)S(1)}, bf16[256,512]{1,0:T(8,128)(2,1)S(1)}, u32[]{:S(2)}, u32[]{:S(2)}) %collective-permute-start.5) | collective-permute-done | bytes 262176 | tf_op jit(solution)/shard_map/ppermute | solution.py:203
  104.2 3.5 %collective-permute-start.18 = (bf16[320,128]{1,0:T(8,128)(2,1)S(1)}, bf16[320,128]{1,0:T(8,128)(2,1)S(1)}, u32[]{:S(2)}, u32[]{:S(2)}) collective-permute-start(bf16[320,128]{1,0:T(8,128)(2,1)S(1)} %get-tuple-element.48), channel_id=1, source_target_pairs={{0,32},{16,48},{32,0},{48,16},{1,33},{17,49},{33,1},{49,17},{2,34}... | collective-permute-start | bytes 245768 | tf_op jit(solution)/shard_map/ppermute | solution.py:203
  112.0 11.8 %all-to-all-start.1 = ((f32[16,1,128]{2,1,0:T(1,128)}), f32[16,1,128]{2,1,0:T(1,128)S(1)}, u32[]{:S(2)}, u32[]{:S(2)}) async-start(f32[16,1,128]{2,1,0:T(1,128)} %broadcast_in_dim.21), calls=%async_computation.1 | async-start | bytes 16384 | tf_op jit(solution)/shard_map/all_to_all | solution.py:286
  125.3 5.3 %all-to-all-done.1 = f32[16,1,128]{2,1,0:T(1,128)S(1)} async-done(((f32[16,1,128]{2,1,0:T(1,128)}), f32[16,1,128]{2,1,0:T(1,128)S(1)}, u32[]{:S(2)}, u32[]{:S(2)}) %all-to-all-start.1) | async-done | bytes 8224 | tf_op jit(solution)/shard_map/all_to_all | solution.py:286
  136.0 4.6 %all-to-all-start.2 = ((bf16[16,48,512]{2,1,0:T(8,128)(2,1)}), bf16[16,48,512]{2,1,0:T(8,128)(2,1)S(1)}, u32[]{:S(2)}, u32[]{:S(2)}) async-start(bf16[16,48,512]{2,1,0:T(8,128)(2,1)} %broadcast_dynamic-update-slice_fusion), calls=%async_computation.2 | async-start | bytes 1572864 | tf_op jit(solution)/shard_map/all_to_all | solution.py:292
  141.3 19.2 %all-to-all-done.2 = bf16[16,48,512]{2,1,0:T(8,128)(2,1)S(1)} async-done(((bf16[16,48,512]{2,1,0:T(8,128)(2,1)}), bf16[16,48,512]{2,1,0:T(8,128)(2,1)S(1)}, u32[]{:S(2)}, u32[]{:S(2)}) %all-to-all-start.2) | async-done | bytes 786464 | tf_op jit(solution)/shard_map/all_to_all | solution.py:292
  167.9 2.5 %collective-permute-done.21 = bf16[128,512]{1,0:T(8,128)(2,1)S(1)} collective-permute-done((bf16[128,512]{1,0:T(8,128)(2,1)S(1)}, bf16[128,512]{1,0:T(8,128)(2,1)S(1)}, u32[]{:S(2)}, u32[]{:S(2)}) %collective-permute-start.21) | collective-permute-done | bytes 131104 | tf_op jit(solution)/shard_map/ppermute | solution.py:203
  172.1 21.6 %all_to_all.20 = bf16[16,32,512]{2,1,0:T(8,128)(2,1)S(1)} all-to-all(bf16[16,32,512]{2,1,0:T(8,128)(2,1)S(1)} %convolution_convert_fusion), channel_id=1, replica_groups=mesh['y_hi'=2,'core'=2,'x'=4,'y_lo'=2,'z'=8] {'y_lo','z'}, dimensions={0} | all-to-all | bytes 1048576 | tf_op jit(solution)/shard_map/all_to_all | solution.py:312
  (74 shorter events, 38.2 us)
Async XLA Ops:
  6.8 9.9 %collective-permute-start = (bf16[16,96,128]{2,1,0:T(8,128)(2,1)S(1)}, bf16[16,96,128]{2,1,0:T(8,128)(2,1)S(1)}, u32[]{:S(2)}, u32[]{:S(2)}) collective-permute-start(bf16[16,96,128]{2,1,0:T(8,128)(2,1)S(1)} %get-tuple-element.28), channel_id=1, source_target_pairs={{0,16},{16,32},{32,48},{48,0},{1,17},{17,33},{33,49},{49,1},{2,18}... | collective-permute-start | bytes 1179656 | tf_op jit(solution)/shard_map/ppermute | solution.py:203
  8.8 9.5 %collective-permute-start.1 = (bf16[16,96,128]{2,1,0:T(8,128)(2,1)S(1)}, bf16[16,96,128]{2,1,0:T(8,128)(2,1)S(1)}, u32[]{:S(2)}, u32[]{:S(2)}) collective-permute-start(bf16[16,96,128]{2,1,0:T(8,128)(2,1)S(1)} %get-tuple-element.29), channel_id=1, source_target_pairs={{0,48},{16,0},{32,16},{48,32},{1,49},{17,1},{33,17},{49,33},{2,50}... | collective-permute-start | bytes 1179656 | tf_op jit(solution)/shard_map/ppermute | solution.py:203
  19.5 18.4 %collective-permute-start.2 = (bf16[16,192,128]{2,1,0:T(8,128)(2,1)S(1)}, bf16[16,192,128]{2,1,0:T(8,128)(2,1)S(1)}, u32[]{:S(2)}, u32[]{:S(2)}) collective-permute-start(bf16[16,192,128]{2,1,0:T(8,128)(2,1)S(1)} %get-tuple-element.30), channel_id=1, source_target_pairs={{0,16},{16,32},{32,48},{48,0},{1,17},{17,33},{33,49},{49,1},{2,18}... | collective-permute-start | bytes 2359304 | tf_op jit(solution)/shard_map/ppermute | solution.py:203
  21.0 17.0 %collective-permute-start.3 = (bf16[16,192,128]{2,1,0:T(8,128)(2,1)S(1)}, bf16[16,192,128]{2,1,0:T(8,128)(2,1)S(1)}, u32[]{:S(2)}, u32[]{:S(2)}) collective-permute-start(bf16[16,192,128]{2,1,0:T(8,128)(2,1)S(1)} %get-tuple-element.31), channel_id=1, source_target_pairs={{0,48},{16,0},{32,16},{48,32},{1,49},{17,1},{33,17},{49,33},{2,50}... | collective-permute-start | bytes 2359304 | tf_op jit(solution)/shard_map/ppermute | solution.py:203
  22.2 29.2 %collective-permute-start.4 = (bf16[416,512]{1,0:T(8,128)(2,1)S(1)}, bf16[416,512]{1,0:T(8,128)(2,1)S(1)}, u32[]{:S(2)}, u32[]{:S(2)}) collective-permute-start(bf16[416,512]{1,0:T(8,128)(2,1)S(1)} %get-tuple-element.33), channel_id=1, source_target_pairs={{0,8},{8,0},{1,9},{9,1},{2,10},{10,2},{3,11},{11,3},{4,12},{12,4},... | collective-permute-start | bytes 1277960 | tf_op jit(solution)/shard_map/ppermute | solution.py:203
  24.0 33.0 %collective-permute-start.8 = (bf16[256,1024]{1,0:T(8,128)(2,1)}, bf16[256,1024]{1,0:T(8,128)(2,1)S(1)}, u32[]{:S(2)}, u32[]{:S(2)}) collective-permute-start(bf16[256,1024]{1,0:T(8,128)(2,1)} %get-tuple-element.37), channel_id=1, source_target_pairs={{0,8},{8,0},{1,9},{9,1},{2,10},{10,2},{3,11},{11,3},{4,12},{12,4},... | collective-permute-start | bytes 1572872 | tf_op jit(solution)/shard_map/ppermute | solution.py:203
  39.9 71.1 %all-to-all-start = ((bf16[16,192,128]{2,1,0:T(8,128)(2,1)}), bf16[16,192,128]{2,1,0:T(8,128)(2,1)S(1)}, u32[]{:S(2)}, u32[]{:S(2)}) async-start(bf16[16,192,128]{2,1,0:T(8,128)(2,1)} %shard_map.106), calls=%async_computation | async-start | bytes 1572864 | tf_op jit(solution)/shard_map/all_to_all | solution.py:238
  50.1 28.0 %collective-permute-start.7 = (bf16[256,1024]{1,0:T(8,128)(2,1)S(1)}, bf16[256,1024]{1,0:T(8,128)(2,1)S(1)}, u32[]{:S(2)}, u32[]{:S(2)}) collective-permute-start(bf16[256,1024]{1,0:T(8,128)(2,1)S(1)} %get-tuple-element.36), channel_id=1, source_target_pairs={{0,8},{8,0},{1,9},{9,1},{2,10},{10,2},{3,11},{11,3},{4,12},{12,4},... | collective-permute-start | bytes 1572872 | tf_op jit(solution)/shard_map/ppermute | solution.py:203
  54.6 17.1 %collective-permute-start.10 = (bf16[4,160,128]{2,1,0:T(8,128)(2,1)S(1)}, bf16[4,160,128]{2,1,0:T(8,128)(2,1)S(1)}, u32[]{:S(2)}, u32[]{:S(2)}) collective-permute-start(bf16[4,160,128]{2,1,0:T(8,128)(2,1)S(1)} %get-tuple-element.39), channel_id=1, source_target_pairs={{0,7},{1,0},{2,1},{3,2},{4,3},{5,4},{6,5},{7,6},{8,15},{9,8},{10,9... | collective-permute-start | bytes 491528 | tf_op jit(solution)/shard_map/ppermute | solution.py:203
  57.0 16.0 %collective-permute-start.9 = (bf16[4,160,128]{2,1,0:T(8,128)(2,1)S(1)}, bf16[4,160,128]{2,1,0:T(8,128)(2,1)S(1)}, u32[]{:S(2)}, u32[]{:S(2)}) collective-permute-start(bf16[4,160,128]{2,1,0:T(8,128)(2,1)S(1)} %get-tuple-element.38), channel_id=1, source_target_pairs={{0,1},{1,2},{2,3},{3,4},{4,5},{5,6},{6,7},{7,0},{8,9},{9,10},{10,1... | collective-permute-start | bytes 491528 | tf_op jit(solution)/shard_map/ppermute | solution.py:203
  74.1 8.7 %collective-permute-start.11 = (bf16[4,320,128]{2,1,0:T(8,128)(2,1)S(1)}, bf16[4,320,128]{2,1,0:T(8,128)(2,1)S(1)}, u32[]{:S(2)}, u32[]{:S(2)}) collective-permute-start(bf16[4,320,128]{2,1,0:T(8,128)(2,1)S(1)} %get-tuple-element.40), channel_id=1, source_target_pairs={{0,1},{1,2},{2,3},{3,4},{4,5},{5,6},{6,7},{7,0},{8,9},{9,10},{10,1... | collective-permute-start | bytes 983048 | tf_op jit(solution)/shard_map/ppermute | solution.py:203
  74.7 8.2 %collective-permute-start.12 = (bf16[4,320,128]{2,1,0:T(8,128)(2,1)S(1)}, bf16[4,320,128]{2,1,0:T(8,128)(2,1)S(1)}, u32[]{:S(2)}, u32[]{:S(2)}) collective-permute-start(bf16[4,320,128]{2,1,0:T(8,128)(2,1)S(1)} %get-tuple-element.41), channel_id=1, source_target_pairs={{0,7},{1,0},{2,1},{3,2},{4,3},{5,4},{6,5},{7,6},{8,15},{9,8},{10,9... | collective-permute-start | bytes 983048 | tf_op jit(solution)/shard_map/ppermute | solution.py:203
  76.9 11.1 %collective-permute-start.6 = (bf16[256,1024]{1,0:T(8,128)(2,1)S(1)}, bf16[256,1024]{1,0:T(8,128)(2,1)S(1)}, u32[]{:S(2)}, u32[]{:S(2)}) collective-permute-start(bf16[256,1024]{1,0:T(8,128)(2,1)S(1)} %get-tuple-element.35), channel_id=1, source_target_pairs={{0,8},{8,0},{1,9},{9,1},{2,10},{10,2},{3,11},{11,3},{4,12},{12,4},... | collective-permute-start | bytes 1572872 | tf_op jit(solution)/shard_map/ppermute | solution.py:203
  84.0 8.1 %collective-permute-start.13 = (bf16[4,320,128]{2,1,0:T(8,128)(2,1)S(1)}, bf16[4,320,128]{2,1,0:T(8,128)(2,1)S(1)}, u32[]{:S(2)}, u32[]{:S(2)}) collective-permute-start(bf16[4,320,128]{2,1,0:T(8,128)(2,1)S(1)} %get-tuple-element.42), channel_id=1, source_target_pairs={{0,1},{1,2},{2,3},{3,4},{4,5},{5,6},{6,7},{7,0},{8,9},{9,10},{10,1... | collective-permute-start | bytes 983048 | tf_op jit(solution)/shard_map/ppermute | solution.py:203
  86.0 6.8 %collective-permute-start.14 = (bf16[4,320,128]{2,1,0:T(8,128)(2,1)S(1)}, bf16[4,320,128]{2,1,0:T(8,128)(2,1)S(1)}, u32[]{:S(2)}, u32[]{:S(2)}) collective-permute-start(bf16[4,320,128]{2,1,0:T(8,128)(2,1)S(1)} %get-tuple-element.43), channel_id=1, source_target_pairs={{0,7},{1,0},{2,1},{3,2},{4,3},{5,4},{6,5},{7,6},{8,15},{9,8},{10,9... | collective-permute-start | bytes 983048 | tf_op jit(solution)/shard_map/ppermute | solution.py:203
  93.8 9.2 %collective-permute-start.15 = (bf16[4,320,128]{2,1,0:T(8,128)(2,1)S(1)}, bf16[4,320,128]{2,1,0:T(8,128)(2,1)S(1)}, u32[]{:S(2)}, u32[]{:S(2)}) collective-permute-start(bf16[4,320,128]{2,1,0:T(8,128)(2,1)S(1)} %get-tuple-element.44), channel_id=1, source_target_pairs={{0,1},{1,2},{2,3},{3,4},{4,5},{5,6},{6,7},{7,0},{8,9},{9,10},{10,1... | collective-permute-start | bytes 983048 | tf_op jit(solution)/shard_map/ppermute | solution.py:203
  94.8 8.3 %collective-permute-start.16 = (bf16[4,320,128]{2,1,0:T(8,128)(2,1)S(1)}, bf16[4,320,128]{2,1,0:T(8,128)(2,1)S(1)}, u32[]{:S(2)}, u32[]{:S(2)}) collective-permute-start(bf16[4,320,128]{2,1,0:T(8,128)(2,1)S(1)} %get-tuple-element.45), channel_id=1, source_target_pairs={{0,7},{1,0},{2,1},{3,2},{4,3},{5,4},{6,5},{7,6},{8,15},{9,8},{10,9... | collective-permute-start | bytes 983048 | tf_op jit(solution)/shard_map/ppermute | solution.py:203
  96.6 5.5 %collective-permute-start.5 = (bf16[256,512]{1,0:T(8,128)(2,1)S(1)}, bf16[256,512]{1,0:T(8,128)(2,1)S(1)}, u32[]{:S(2)}, u32[]{:S(2)}) collective-permute-start(bf16[256,512]{1,0:T(8,128)(2,1)S(1)} %copy-done.7), channel_id=1, source_target_pairs={{0,8},{8,0},{1,9},{9,1},{2,10},{10,2},{3,11},{11,3},{4,12},{12,4},... | collective-permute-start | bytes 786440 | tf_op jit(solution)/shard_map/ppermute | solution.py:203
  103.7 4.9 %collective-permute-start.17 = (bf16[320,128]{1,0:T(8,128)(2,1)S(1)}, bf16[320,128]{1,0:T(8,128)(2,1)S(1)}, u32[]{:S(2)}, u32[]{:S(2)}) collective-permute-start(bf16[320,128]{1,0:T(8,128)(2,1)S(1)} %get-tuple-element.47), channel_id=1, source_target_pairs={{0,16},{16,32},{32,48},{48,0},{1,17},{17,33},{33,49},{49,1},{2,18}... | collective-permute-start | bytes 245768 | tf_op jit(solution)/shard_map/ppermute | solution.py:203
  104.2 6.2 %collective-permute-start.18 = (bf16[320,128]{1,0:T(8,128)(2,1)S(1)}, bf16[320,128]{1,0:T(8,128)(2,1)S(1)}, u32[]{:S(2)}, u32[]{:S(2)}) collective-permute-start(bf16[320,128]{1,0:T(8,128)(2,1)S(1)} %get-tuple-element.48), channel_id=1, source_target_pairs={{0,32},{16,48},{32,0},{48,16},{1,33},{17,49},{33,1},{49,17},{2,34}... | collective-permute-start | bytes 245768 | tf_op jit(solution)/shard_map/ppermute | solution.py:203
  112.0 18.7 %all-to-all-start.1 = ((f32[16,1,128]{2,1,0:T(1,128)}), f32[16,1,128]{2,1,0:T(1,128)S(1)}, u32[]{:S(2)}, u32[]{:S(2)}) async-start(f32[16,1,128]{2,1,0:T(1,128)} %broadcast_in_dim.21), calls=%async_computation.1 | async-start | bytes 16384 | tf_op jit(solution)/shard_map/all_to_all | solution.py:286
  136.0 24.5 %all-to-all-start.2 = ((bf16[16,48,512]{2,1,0:T(8,128)(2,1)}), bf16[16,48,512]{2,1,0:T(8,128)(2,1)S(1)}, u32[]{:S(2)}, u32[]{:S(2)}) async-start(bf16[16,48,512]{2,1,0:T(8,128)(2,1)} %broadcast_dynamic-update-slice_fusion), calls=%async_computation.2 | async-start | bytes 1572864 | tf_op jit(solution)/shard_map/all_to_all | solution.py:292
  164.9 5.4 %collective-permute-start.21 = (bf16[128,512]{1,0:T(8,128)(2,1)S(1)}, bf16[128,512]{1,0:T(8,128)(2,1)S(1)}, u32[]{:S(2)}, u32[]{:S(2)}) collective-permute-start(bf16[128,512]{1,0:T(8,128)(2,1)S(1)} %get-tuple-element.52), channel_id=1, source_target_pairs={{0,32},{16,48},{32,0},{48,16},{1,33},{17,49},{33,1},{49,17},{2,34}... | collective-permute-start | bytes 393224 | tf_op jit(solution)/shard_map/ppermute | solution.py:203
  166.1 5.5 %collective-permute-start.22 = (bf16[128,512]{1,0:T(8,128)(2,1)S(1)}, bf16[128,512]{1,0:T(8,128)(2,1)S(1)}, u32[]{:S(2)}, u32[]{:S(2)}) collective-permute-start(bf16[128,512]{1,0:T(8,128)(2,1)S(1)} %get-tuple-element.52), channel_id=1, source_target_pairs={{0,16},{16,32},{32,48},{48,0},{1,17},{17,33},{33,49},{49,1},{2,18}... | collective-permute-start | bytes 393224 | tf_op jit(solution)/shard_map/ppermute | solution.py:203
  (13 other events, 280.9 us)

commit v4 on v2

v4 whole, which is shorter than its diff:
```python
import functools
import math

import jax
import jax.numpy as jnp
from jax import lax
from jax.experimental import pallas as pl
from jax.experimental.pallas import tpu as pltpu
from jax.sharding import Mesh
from jax.sharding import PartitionSpec as P

DP = ("x", "y_lo", "z")
YZ = ("y_lo", "z")
SECTION = ("y_hi", "core")
EVERY = SECTION + DP

NX, NY, NZ = 4, 2, 8
TAILS = 4


beta_one = 0.9
beta_two = 0.95
correct_one = 1.0 - 0.9**20
correct_two = 1.0 - 0.95**20
adam_eps = 1e-08
decay_rate = 0.1
learn_rate = 0.1

f32 = jnp.float32
bf16 = jnp.bfloat16

ROWS = 128
COLS = 512
HALF = COLS // 2
Z_WIDE = NX * ROWS


def column(x, y, z):
    return pl.multiple_of((x * (NY * NZ) + y * NZ + z) * ROWS, ROWS)


def side_columns(where, side, away, acts, turn=0):
    owner = lax.rem(where[1] + away, NZ)
    xs = [lax.rem(turn + k, NX) for k in range(NX)]
    return jnp.concatenate([acts[:, pl.ds(column(x, side, owner), ROWS)] for x in xs], axis=1)


def partner_pairs(joined):
    tail = joined[joined.shape[1] // 2 :, :]
    half = tail.shape[1] // 2
    return jnp.concatenate([tail[:, :half], tail[:, half:]], axis=0)


def z_terms(where, away, pairs, acts, joined, part):
    own = jnp.dot(
        pairs[...], side_columns(where, where[2], away, acts), preferred_element_type=f32
    )
    term = own + jnp.dot(partner_pairs(joined), part, preferred_element_type=f32)
    for k in range(NX):
        yield k, term[:, k * ROWS : (k + 1) * ROWS]


def first_kernel(where, tails, *refs):
    acts, (pairs, give, placed) = refs[:NX], refs[NX:]
    tail = tails.shape[0] // TAILS

    def place(t, carry):
        src = pl.ds(pl.multiple_of(t * tail, tail), tail)
        dst = pl.ds(pl.multiple_of(where[3 + t] * tail, tail), tail)
        placed[dst, :] = tails[src, :]
        return carry

    lax.fori_loop(0, TAILS, place, 0)
    tokens = tails.shape[0]
    value = placed[...].astype(f32).T.astype(bf16)
    pairs[...] = value
    for k in range(NX):
        give[:tokens, k * ROWS : (k + 1) * ROWS] = acts[k][...]
    give[tokens:, :tokens] = value[:HALF]
    give[tokens:, tokens:] = value[HALF:]


def pack_kernel(where, acts, *gives):
    for k, give in enumerate(gives):
        away = NZ // 2 - 1 - k
        for n, far in enumerate((away, NZ - away) if away else (0,)):
            give[:, n * Z_WIDE : (n + 1) * Z_WIDE] = side_columns(where, 1 - where[2], far, acts)


def first_z_kernel(where, pairs, acts, joined, out_p, out_m):
    part = joined[: acts.shape[0], :]
    for k, term in z_terms(where, NZ // 2, pairs, acts, joined, part):
        out_p[k] = term[:HALF].astype(bf16)
        out_m[k] = term[HALF:].astype(bf16)


def later_z_kernel(s, where, pairs, acts, joined, part, got_p, got_m, out_p, out_m):
    away = NZ // 2 - s
    for k, term in z_terms(where, away, pairs, acts, joined, part[:, :Z_WIDE]):
        if s == 1:
            out_p[k, :HALF] = (term[:HALF] + got_p[k].astype(f32)).astype(bf16)
            out_p[k, HALF:] = term[HALF:].astype(bf16)
        else:
            out_p[k] = (term + got_p[k].astype(f32)).astype(bf16)
    for k, term in z_terms(where, NZ - away, pairs, acts, joined, part[:, Z_WIDE:]):
        if s == 1:
            out_m[k, :HALF] = term[:HALF].astype(bf16)
            out_m[k, HALF:] = (term[HALF:] + got_m[k].astype(f32)).astype(bf16)
        else:
            out_m[k] = (term + got_m[k].astype(f32)).astype(bf16)


def own_z_kernel(where, pairs, acts, joined, part, out):
    mine = jnp.dot(
        pairs[...], side_columns(where, where[2], 0, acts, where[0]), preferred_element_type=f32
    )
    xs = [lax.rem(where[0] + r, NX) for r in range(NX)]
    parts = [part[:, pl.ds(pl.multiple_of(x * ROWS, ROWS), ROWS)] for x in xs]
    out[...] = mine + jnp.dot(
        partner_pairs(joined), jnp.concatenate(parts, axis=1), preferred_element_type=f32
    )


def last_z_kernel(where, term, got_p, got_m, own, *sends):
    for r in range(NX):
        x = lax.rem(where[0] + r, NX)
        total = term[:, r * ROWS : (r + 1) * ROWS] + got_p[x].astype(f32) + got_m[x].astype(f32)
        if r == 0:
            own[...] = total
        else:
            sends[r - 1][...] = total.astype(bf16)


def gradient_kernel(scale, overflow, own, *refs):
    gots, (grad, squares) = refs[: NX - 1], refs[NX - 1 :]
    total = own[...]
    for got in gots:
        total += got[...].astype(f32)
    total = total.T * scale
    grad[...] = total
    kept = jnp.where(overflow[0, 0] == 0, 1.0, 0.0)
    squares[...] = jnp.broadcast_to(jnp.sum(total * total) * kept, squares.shape)


def tokens_kernel(where, mine, out):
    for r in range(NX):
        owner = lax.rem(where[0] + r, NX)
        for g in range(NY * NZ):
            start = pl.multiple_of((owner * (NY * NZ) + g) * ROWS, ROWS)
            out[g, :, r * ROWS : (r + 1) * ROWS] = mine[:, pl.ds(start, ROWS)]


def near(x):
    return pltpu.with_memory_space_constraint(x, pltpu.VMEM)


SCALARS = pl.BlockSpec(memory_space=pltpu.SMEM)
GRANT = pltpu.CompilerParams(vmem_limit_bytes=8 * 2**20)
NEAR = pl.BlockSpec(memory_space=pltpu.VMEM)


def on_core(kernel, scalars, arrays, outs, scratch=()):
    return pl.pallas_call(
        kernel,
        in_specs=[SCALARS] * len(scalars) + [NEAR] * len(arrays),
        out_specs=[NEAR] * len(outs),
        out_shape=list(outs),
        scratch_shapes=scratch,
        compiler_params=GRANT,
    )(*scalars, *[near(a) for a in arrays])


def shift(x, axis, n, by):
    return lax.ppermute(x, axis, [(i, (i + by) % n) for i in range(n)])


def both(plus, minus, axis, n):
    return shift(plus, axis, n, 1), shift(minus, axis, n, -1)


def swap_side(x):
    return shift(x, "y_lo", NY, 1)


def first_terms(where, tails, acts):
    tokens = tails.shape[0]
    block = lambda x: lambda i, w: (
        0,
        x * (NY * NZ) + (1 - w[2]) * NZ + lax.rem(w[1] + NZ // 2, NZ),
    )
    whole = lambda *shape: pl.BlockSpec(shape, lambda i, w: (0, 0))
    shapes = (COLS, tokens), (2 * tokens, Z_WIDE)
    return pl.pallas_call(
        first_kernel,
        grid_spec=pltpu.PrefetchScalarGridSpec(
            num_scalar_prefetch=1,
            grid=(1,),
            in_specs=[whole(*tails.shape)]
            + [pl.BlockSpec((tokens, ROWS), block(x)) for x in range(NX)],
            out_specs=[whole(*shape) for shape in shapes],
            scratch_shapes=[pltpu.VMEM(tails.shape, bf16)],
        ),
        out_shape=[jax.ShapeDtypeStruct(shape, bf16) for shape in shapes],
        compiler_params=GRANT,
        name="work_first",
    )(where, tails, *([acts] * NX))


def sum_terms(where, tails, acts):
    tokens = acts.shape[0]
    two = lambda *shape: [pltpu.VMEM(shape, bf16)] * 2
    z_pairs, give = first_terms(where, tails, acts)
    wide = [2 * Z_WIDE] * (NZ // 2 - 1) + [Z_WIDE]
    gives = on_core(pack_kernel, [where], [acts], [pltpu.VMEM((tokens, w), bf16) for w in wide])
    joined, *parts = [swap_side(g) for g in [give, *gives]]

    sends = on_core(first_z_kernel, [where], [z_pairs, acts, joined], two(NX, HALF, ROWS))
    gots = both(*sends, "z", NZ)
    for s in range(1, NZ // 2):
        sends = on_core(
            functools.partial(later_z_kernel, s),
            [where],
            [z_pairs, acts, joined, parts[s - 1], *gots],
            two(NX, COLS, ROWS),
        )
        gots = both(*sends, "z", NZ)
    piece = lambda t: pltpu.VMEM((COLS, ROWS), t)
    (term,) = on_core(
        own_z_kernel, [where], [z_pairs, acts, joined, parts[-1]], [pltpu.VMEM((COLS, Z_WIDE), f32)]
    )
    own, *sends = on_core(
        last_z_kernel, [where], [term, *gots], [piece(f32)] + [piece(bf16)] * (NX - 1)
    )
    gots = [shift(send, "x", NX, r + 1) for r, send in enumerate(sends)]
    return own, gots


def local(
    activations, tail_grads, tail_slots, master, moment1, moment2, overflow, clip_on, next_inputs
):
    acts = activations[0]
    tails = tail_grads[0]
    tok_dev, width = acts.shape
    toks = next_inputs.shape[1]
    where = jnp.stack([lax.axis_index(a) for a in ("x", "z", "y_lo")]).astype(jnp.int32)
    where = jnp.concatenate([where, tail_slots[0, 0]])

    tokens = jax.ShapeDtypeStruct((NY * NZ, toks, NX * ROWS), bf16)
    (tokens,) = on_core(tokens_kernel, [where], [next_inputs[0]], [tokens])
    tokens = lax.all_to_all(tokens, YZ, 0, 0, tiled=True)

    own, gots = sum_terms(where, tails, acts)
    gradient, part_sq = on_core(
        functools.partial(gradient_kernel, 1.0 / (tok_dev * NX * NY * NZ)),
        [overflow],
        [own, *gots],
        [pltpu.VMEM((ROWS, COLS), f32), pltpu.VMEM((1, ROWS), f32)],
    )
    keep = (overflow[0, 0] == 0).astype(f32)
    for axes in (("y_hi", "core", "x"), YZ):
        part_sq = jnp.broadcast_to(part_sq[None], (4 * NX, 1, ROWS))
        part_sq = jnp.sum(lax.all_to_all(part_sq, axes, 0, 0, tiled=True), axis=0)
    sumsq = part_sq[0, 0]
    norm_value = jnp.sqrt(sumsq)
    factor = jnp.where(clip_on[0] == 1, 1.0 / jnp.maximum(norm_value, 1.0), 1.0)
    clipped = gradient * factor
    old_master = master[0]
    m_next = beta_one * moment1[0] + (1.0 - beta_one) * clipped
    v_next = beta_two * moment2[0] + (1.0 - beta_two) * (clipped * clipped)
    update = (
        m_next / correct_one / (jnp.sqrt(v_next / correct_two) + adam_eps) + decay_rate * old_master
    )
    updated = jnp.where(keep > 0.5, old_master - learn_rate * update, old_master)
    weights = updated.astype(bf16)

    along_x = jnp.concatenate(
        [weights] + [shift(weights, "x", NX, -r) for r in range(1, NX)], axis=0
    )
    partial = jnp.einsum("gtk,kc->gtc", tokens, along_x, preferred_element_type=f32).astype(bf16)
    parts = lax.all_to_all(partial, YZ, 0, 0, tiled=True)
    result = jnp.sum(parts.astype(f32), axis=0)
    next_out = (result * (1.0 / math.sqrt(width))).astype(bf16)
    return (updated[None], next_out[None])


def solution(mesh):
    finer = Mesh(mesh.devices.reshape(2, 2, NX, NY, NZ), EVERY)
    return jax.shard_map(
        local,
        mesh=finer,
        in_specs=(
            P(SECTION, DP, None),
            P(SECTION, DP, None),
            P(SECTION, DP, None),
            P(SECTION, DP, None),
            P(SECTION, DP, None),
            P(SECTION, DP, None),
            P(SECTION, DP),
            P(SECTION),
            P(SECTION, DP, None),
        ),
        out_specs=(P(SECTION, DP, None), P(SECTION, DP, None)),
        check_vma=False,
    )
```

time: 179 us -> 154 us (0.86)
  the two profiles are of different devices: /device:TPU:40 before, /device:TPU:1 now
where the time goes in v4:
time: 154 us; the launch traced here: 152 us
  waiting for transfers between devices  51.3 us (33%)
  starting transfers between devices  42 us (27%)
  blocking collectives  39.5 us (26%)
  Pallas kernels  10.3 us (7%)
  local copies, waits for them, and re-layouts  3.77 us (2%)
  other arithmetic  2.41 us (2%)
  between operations  2.26 us (1%)
    ppermute x19, waiting for transfers between devices, shift(): return lax.ppermute(x, axis, [(i, (i + by) % n) for i in range(n)])  36.6 us
    ppermute x19, starting transfers between devices, shift(): return lax.ppermute(x, axis, [(i, (i + by) % n) for i in range(n)])  33.3 us
    all_to_all x1, blocking collectives, local(): part_sq = jnp.sum(lax.all_to_all(part_sq, axes, 0, 0, tiled=True), axis=0)  20.6 us
    all_to_all x1, blocking collectives, local(): parts = lax.all_to_all(partial, YZ, 0, 0, tiled=True)  18.9 us
    pallas_call x9, Pallas kernels, on_core(): pl.pallas_call(kernel, in_specs=[SCALARS] * len(scalars) + [NEAR] * len(a...  9.46 us
    all_to_all x1, waiting for transfers between devices, local(): tokens = lax.all_to_all(tokens, YZ, 0, 0, tiled=True)  8.98 us
    all_to_all x1, waiting for transfers between devices, local(): part_sq = jnp.sum(lax.all_to_all(part_sq, axes, 0, 0, tiled=True), axis=0)  5.74 us
    all_to_all x1, starting transfers between devices, local(): part_sq = jnp.sum(lax.all_to_all(part_sq, axes, 0, 0, tiled=True), axis=0)  5.17 us
  transfers between devices with their start and end apart: 21, of which 14 were waited for; matrix products, arithmetic and copies ran while one was open for 1% of the time, Pallas kernels for 5%

profile of v4, /device:TPU:1, one launch (start us, length us, event | category | flops | bytes accessed | tf_op | source)
XLA Modules:
  0.0 152.0 jit_solution(5313874667762530712)
XLA Ops:
  1.4 2.2 %copy-done = bf16[1,256,8192]{2,1,0:T(8,128)(2,1)S(1)} copy-done((bf16[1,256,8192]{2,1,0:T(8,128)(2,1)S(1)}, bf16[1,256,8192]{2,1,0:T(8,128)(2,1)}, u32[]{:S(2)}) %copy-start) | copy-done | bytes 4194328
  5.3 2.2 %collective-permute-start = (bf16[512,512]{1,0:T(8,128)(2,1)S(1)}, bf16[512,512]{1,0:T(8,128)(2,1)S(1)}, u32[]{:S(2)}, u32[]{:S(2)}) collective-permute-start(bf16[512,512]{1,0:T(8,128)(2,1)S(1)} %get-tuple-element.23), channel_id=1, source_target_pairs={{0,8},{8,0},{1,9},{9,1},{2,10},{10,2},{3,11},{11,3},{4,12},{12,4},... | collective-permute-start | bytes 1572872 | tf_op jit(solution)/shard_map/ppermute | solution.py:174
  10.0 8.0 %collective-permute-done.joined = bf16[512,512]{1,0:T(8,128)(2,1)S(1)} collective-permute-done((bf16[512,512]{1,0:T(8,128)(2,1)S(1)}, bf16[512,512]{1,0:T(8,128)(2,1)S(1)}, u32[]{:S(2)}, u32[]{:S(2)}) %collective-permute-start) | collective-permute-done | bytes 524320 | tf_op jit(solution)/shard_map/ppermute | solution.py:174
  19.0 2.8 %collective-permute-start.5 = (bf16[4,256,128]{2,1,0:T(8,128)(2,1)S(1)}, bf16[4,256,128]{2,1,0:T(8,128)(2,1)S(1)}, u32[]{:S(2)}, u32[]{:S(2)}) collective-permute-start(bf16[4,256,128]{2,1,0:T(8,128)(2,1)S(1)} %get-tuple-element.28), channel_id=1, source_target_pairs={{0,1},{1,2},{2,3},{3,4},{4,5},{5,6},{6,7},{7,0},{8,9},{9,10},{10,1... | collective-permute-start | bytes 786440 | tf_op jit(solution)/shard_map/ppermute | solution.py:174
  21.7 4.0 %collective-permute-start.6 = (bf16[4,256,128]{2,1,0:T(8,128)(2,1)S(1)}, bf16[4,256,128]{2,1,0:T(8,128)(2,1)S(1)}, u32[]{:S(2)}, u32[]{:S(2)}) collective-permute-start(bf16[4,256,128]{2,1,0:T(8,128)(2,1)S(1)} %get-tuple-element.29), channel_id=1, source_target_pairs={{0,7},{1,0},{2,1},{3,2},{4,3},{5,4},{6,5},{7,6},{8,15},{9,8},{10,9... | collective-permute-start | bytes 786440 | tf_op jit(solution)/shard_map/ppermute | solution.py:174
  27.1 2.2 %collective-permute-done.4.part = bf16[256,1024]{1,0:T(8,128)(2,1)S(1)} collective-permute-done((bf16[256,1024]{1,0:T(8,128)(2,1)S(1)}, bf16[256,1024]{1,0:T(8,128)(2,1)S(1)}, u32[]{:S(2)}, u32[]{:S(2)}) %collective-permute-start.4) | collective-permute-done | bytes 524320 | tf_op jit(solution)/shard_map/ppermute | solution.py:174
  30.8 2.5 %collective-permute-start.7 = (bf16[4,512,128]{2,1,0:T(8,128)(2,1)S(1)}, bf16[4,512,128]{2,1,0:T(8,128)(2,1)S(1)}, u32[]{:S(2)}, u32[]{:S(2)}) collective-permute-start(bf16[4,512,128]{2,1,0:T(8,128)(2,1)S(1)} %get-tuple-element.30), channel_id=1, source_target_pairs={{0,1},{1,2},{2,3},{3,4},{4,5},{5,6},{6,7},{7,0},{8,9},{9,10},{10,1... | collective-permute-start | bytes 1572872 | tf_op jit(solution)/shard_map/ppermute | solution.py:174
  33.3 4.0 %collective-permute-start.8 = (bf16[4,512,128]{2,1,0:T(8,128)(2,1)S(1)}, bf16[4,512,128]{2,1,0:T(8,128)(2,1)S(1)}, u32[]{:S(2)}, u32[]{:S(2)}) collective-permute-start(bf16[4,512,128]{2,1,0:T(8,128)(2,1)S(1)} %get-tuple-element.31), channel_id=1, source_target_pairs={{0,7},{1,0},{2,1},{3,2},{4,3},{5,4},{6,5},{7,6},{8,15},{9,8},{10,9... | collective-permute-start | bytes 1572872 | tf_op jit(solution)/shard_map/ppermute | solution.py:174
  38.6 1.8 %collective-permute-done.3.part = bf16[256,1024]{1,0:T(8,128)(2,1)S(1)} collective-permute-done((bf16[256,1024]{1,0:T(8,128)(2,1)S(1)}, bf16[256,1024]{1,0:T(8,128)(2,1)S(1)}, u32[]{:S(2)}, u32[]{:S(2)}) %collective-permute-start.3) | collective-permute-done | bytes 524320 | tf_op jit(solution)/shard_map/ppermute | solution.py:174
  40.5 6.4 %collective-permute-done.7.got_p = bf16[4,512,128]{2,1,0:T(8,128)(2,1)S(1)} collective-permute-done((bf16[4,512,128]{2,1,0:T(8,128)(2,1)S(1)}, bf16[4,512,128]{2,1,0:T(8,128)(2,1)S(1)}, u32[]{:S(2)}, u32[]{:S(2)}) %collective-permute-start.7) | collective-permute-done | bytes 524320 | tf_op jit(solution)/shard_map/ppermute | solution.py:174
  48.2 2.6 %collective-permute-start.10 = (bf16[4,512,128]{2,1,0:T(8,128)(2,1)S(1)}, bf16[4,512,128]{2,1,0:T(8,128)(2,1)S(1)}, u32[]{:S(2)}, u32[]{:S(2)}) collective-permute-start(bf16[4,512,128]{2,1,0:T(8,128)(2,1)S(1)} %get-tuple-element.33), channel_id=1, source_target_pairs={{0,7},{1,0},{2,1},{3,2},{4,3},{5,4},{6,5},{7,6},{8,15},{9,8},{10,9... | collective-permute-start | bytes 1572872 | tf_op jit(solution)/shard_map/ppermute | solution.py:174
  51.7 6.8 %collective-permute-done.10.got_m = bf16[4,512,128]{2,1,0:T(8,128)(2,1)S(1)} collective-permute-done((bf16[4,512,128]{2,1,0:T(8,128)(2,1)S(1)}, bf16[4,512,128]{2,1,0:T(8,128)(2,1)S(1)}, u32[]{:S(2)}, u32[]{:S(2)}) %collective-permute-start.10) | collective-permute-done | bytes 524320 | tf_op jit(solution)/shard_map/ppermute | solution.py:174
  58.5 3.1 %collective-permute-done.9.got_p = bf16[4,512,128]{2,1,0:T(8,128)(2,1)S(1)} collective-permute-done((bf16[4,512,128]{2,1,0:T(8,128)(2,1)S(1)}, bf16[4,512,128]{2,1,0:T(8,128)(2,1)S(1)}, u32[]{:S(2)}, u32[]{:S(2)}) %collective-permute-start.9) | collective-permute-done | bytes 524320 | tf_op jit(solution)/shard_map/ppermute | solution.py:174
  63.1 2.7 %collective-permute-start.12 = (bf16[4,512,128]{2,1,0:T(8,128)(2,1)S(1)}, bf16[4,512,128]{2,1,0:T(8,128)(2,1)S(1)}, u32[]{:S(2)}, u32[]{:S(2)}) collective-permute-start(bf16[4,512,128]{2,1,0:T(8,128)(2,1)S(1)} %get-tuple-element.35), channel_id=1, source_target_pairs={{0,7},{1,0},{2,1},{3,2},{4,3},{5,4},{6,5},{7,6},{8,15},{9,8},{10,9... | collective-permute-start | bytes 1572872 | tf_op jit(solution)/shard_map/ppermute | solution.py:174
  67.1 4.3 %collective-permute-done.1.part = bf16[256,512]{1,0:T(8,128)(2,1)S(1)} collective-permute-done((bf16[256,512]{1,0:T(8,128)(2,1)S(1)}, bf16[256,512]{1,0:T(8,128)(2,1)S(1)}, u32[]{:S(2)}, u32[]{:S(2)}) %collective-permute-start.1) | collective-permute-done | bytes 262176 | tf_op jit(solution)/shard_map/ppermute | solution.py:174
  75.3 2.5 %collective-permute-start.14 = (bf16[512,128]{1,0:T(8,128)(2,1)S(1)}, bf16[512,128]{1,0:T(8,128)(2,1)S(1)}, u32[]{:S(2)}, u32[]{:S(2)}) collective-permute-start(bf16[512,128]{1,0:T(8,128)(2,1)S(1)} %get-tuple-element.38), channel_id=1, source_target_pairs={{0,32},{16,48},{32,0},{48,16},{1,33},{17,49},{33,1},{49,17},{2,34}... | collective-permute-start | bytes 393224 | tf_op jit(solution)/shard_map/ppermute | solution.py:174
  79.5 1.9 %collective-permute-done.14.refs_1_ = bf16[512,128]{1,0:T(8,128)(2,1)S(1)} collective-permute-done((bf16[512,128]{1,0:T(8,128)(2,1)S(1)}, bf16[512,128]{1,0:T(8,128)(2,1)S(1)}, u32[]{:S(2)}, u32[]{:S(2)}) %collective-permute-start.14) | collective-permute-done | bytes 131104 | tf_op jit(solution)/shard_map/ppermute | solution.py:174
  81.9 20.6 %all_to_all.20 = f32[16,1,128]{2,1,0:T(1,128)S(1)} all-to-all(f32[16,1,128]{2,1,0:T(1,128)S(1)} %broadcast_in_dim.9), channel_id=1, replica_groups=mesh['y_hi'=2,'core'=2,'x'=4,'y_lo'=2,'z'=8] {'y_hi','core','x'}, dimensions={0} | all-to-all | bytes 16384 | tf_op jit(solution)/shard_map/all_to_all | solution.py:262
  103.0 5.2 %all-to-all-start.1 = ((f32[16,1,128]{2,1,0:T(1,128)}), f32[16,1,128]{2,1,0:T(1,128)S(1)}, u32[]{:S(2)}, u32[]{:S(2)}) async-start(f32[16,1,128]{2,1,0:T(1,128)} %broadcast_in_dim.20), calls=%async_computation.1 | async-start | bytes 16384 | tf_op jit(solution)/shard_map/all_to_all | solution.py:262
  108.2 1.5 shard_map.112
  109.7 5.7 %all-to-all-done.1 = f32[16,1,128]{2,1,0:T(1,128)S(1)} async-done(((f32[16,1,128]{2,1,0:T(1,128)}), f32[16,1,128]{2,1,0:T(1,128)S(1)}, u32[]{:S(2)}, u32[]{:S(2)}) %all-to-all-start.1) | async-done | bytes 8224 | tf_op jit(solution)/shard_map/all_to_all | solution.py:262
  115.5 3.6 %all-to-all-start.2 = ((bf16[16,32,512]{2,1,0:T(8,128)(2,1)}), bf16[16,32,512]{2,1,0:T(8,128)(2,1)S(1)}, u32[]{:S(2)}, u32[]{:S(2)}) async-start(bf16[16,32,512]{2,1,0:T(8,128)(2,1)} %shard_map.112), calls=%async_computation.2 | async-start | bytes 1048576 | tf_op jit(solution)/shard_map/all_to_all | solution.py:250
  122.9 9.0 %all-to-all-done.2 = bf16[16,32,512]{2,1,0:T(8,128)(2,1)S(1)} async-done(((bf16[16,32,512]{2,1,0:T(8,128)(2,1)}), bf16[16,32,512]{2,1,0:T(8,128)(2,1)S(1)}, u32[]{:S(2)}, u32[]{:S(2)}) %all-to-all-start.2) | async-done | bytes 524320 | tf_op jit(solution)/shard_map/all_to_all | solution.py:250
  132.3 18.9 %all_to_all.21 = bf16[16,32,512]{2,1,0:T(8,128)(2,1)S(1)} all-to-all(bf16[16,32,512]{2,1,0:T(8,128)(2,1)S(1)} %convolution_convert_fusion), channel_id=1, replica_groups=mesh['y_hi'=2,'core'=2,'x'=4,'y_lo'=2,'z'=8] {'y_lo','z'}, dimensions={0} | all-to-all | bytes 1048576 | tf_op jit(solution)/shard_map/all_to_all | solution.py:280
  (53 shorter events, 25.2 us)
Async XLA Ops:
  5.3 12.7 %collective-permute-start = (bf16[512,512]{1,0:T(8,128)(2,1)S(1)}, bf16[512,512]{1,0:T(8,128)(2,1)S(1)}, u32[]{:S(2)}, u32[]{:S(2)}) collective-permute-start(bf16[512,512]{1,0:T(8,128)(2,1)S(1)} %get-tuple-element.23), channel_id=1, source_target_pairs={{0,8},{8,0},{1,9},{9,1},{2,10},{10,2},{3,11},{11,3},{4,12},{12,4},... | collective-permute-start | bytes 1572872 | tf_op jit(solution)/shard_map/ppermute | solution.py:174
  8.6 20.6 %collective-permute-start.4 = (bf16[256,1024]{1,0:T(8,128)(2,1)S(1)}, bf16[256,1024]{1,0:T(8,128)(2,1)S(1)}, u32[]{:S(2)}, u32[]{:S(2)}) collective-permute-start(bf16[256,1024]{1,0:T(8,128)(2,1)S(1)} %get-tuple-element.27), channel_id=1, source_target_pairs={{0,8},{8,0},{1,9},{9,1},{2,10},{10,2},{3,11},{11,3},{4,12},{12,4},... | collective-permute-start | bytes 1572872 | tf_op jit(solution)/shard_map/ppermute | solution.py:174
  19.0 10.5 %collective-permute-start.5 = (bf16[4,256,128]{2,1,0:T(8,128)(2,1)S(1)}, bf16[4,256,128]{2,1,0:T(8,128)(2,1)S(1)}, u32[]{:S(2)}, u32[]{:S(2)}) collective-permute-start(bf16[4,256,128]{2,1,0:T(8,128)(2,1)S(1)} %get-tuple-element.28), channel_id=1, source_target_pairs={{0,1},{1,2},{2,3},{3,4},{4,5},{5,6},{6,7},{7,0},{8,9},{9,10},{10,1... | collective-permute-start | bytes 786440 | tf_op jit(solution)/shard_map/ppermute | solution.py:174
  21.7 7.7 %collective-permute-start.6 = (bf16[4,256,128]{2,1,0:T(8,128)(2,1)S(1)}, bf16[4,256,128]{2,1,0:T(8,128)(2,1)S(1)}, u32[]{:S(2)}, u32[]{:S(2)}) collective-permute-start(bf16[4,256,128]{2,1,0:T(8,128)(2,1)S(1)} %get-tuple-element.29), channel_id=1, source_target_pairs={{0,7},{1,0},{2,1},{3,2},{4,3},{5,4},{6,5},{7,6},{8,15},{9,8},{10,9... | collective-permute-start | bytes 786440 | tf_op jit(solution)/shard_map/ppermute | solution.py:174
  25.8 14.7 %collective-permute-start.3 = (bf16[256,1024]{1,0:T(8,128)(2,1)S(1)}, bf16[256,1024]{1,0:T(8,128)(2,1)S(1)}, u32[]{:S(2)}, u32[]{:S(2)}) collective-permute-start(bf16[256,1024]{1,0:T(8,128)(2,1)S(1)} %get-tuple-element.26), channel_id=1, source_target_pairs={{0,8},{8,0},{1,9},{9,1},{2,10},{10,2},{3,11},{11,3},{4,12},{12,4},... | collective-permute-start | bytes 1572872 | tf_op jit(solution)/shard_map/ppermute | solution.py:174
  30.8 16.1 %collective-permute-start.7 = (bf16[4,512,128]{2,1,0:T(8,128)(2,1)S(1)}, bf16[4,512,128]{2,1,0:T(8,128)(2,1)S(1)}, u32[]{:S(2)}, u32[]{:S(2)}) collective-permute-start(bf16[4,512,128]{2,1,0:T(8,128)(2,1)S(1)} %get-tuple-element.30), channel_id=1, source_target_pairs={{0,1},{1,2},{2,3},{3,4},{4,5},{5,6},{6,7},{7,0},{8,9},{9,10},{10,1... | collective-permute-start | bytes 1572872 | tf_op jit(solution)/shard_map/ppermute | solution.py:174
  33.3 13.6 %collective-permute-start.8 = (bf16[4,512,128]{2,1,0:T(8,128)(2,1)S(1)}, bf16[4,512,128]{2,1,0:T(8,128)(2,1)S(1)}, u32[]{:S(2)}, u32[]{:S(2)}) collective-permute-start(bf16[4,512,128]{2,1,0:T(8,128)(2,1)S(1)} %get-tuple-element.31), channel_id=1, source_target_pairs={{0,7},{1,0},{2,1},{3,2},{4,3},{5,4},{6,5},{7,6},{8,15},{9,8},{10,9... | collective-permute-start | bytes 1572872 | tf_op jit(solution)/shard_map/ppermute | solution.py:174
  37.3 14.4 %collective-permute-start.2 = (bf16[256,1024]{1,0:T(8,128)(2,1)S(1)}, bf16[256,1024]{1,0:T(8,128)(2,1)S(1)}, u32[]{:S(2)}, u32[]{:S(2)}) collective-permute-start(bf16[256,1024]{1,0:T(8,128)(2,1)S(1)} %get-tuple-element.25), channel_id=1, source_target_pairs={{0,8},{8,0},{1,9},{9,1},{2,10},{10,2},{3,11},{11,3},{4,12},{12,4},... | collective-permute-start | bytes 1572872 | tf_op jit(solution)/shard_map/ppermute | solution.py:174
  48.2 10.4 %collective-permute-start.10 = (bf16[4,512,128]{2,1,0:T(8,128)(2,1)S(1)}, bf16[4,512,128]{2,1,0:T(8,128)(2,1)S(1)}, u32[]{:S(2)}, u32[]{:S(2)}) collective-permute-start(bf16[4,512,128]{2,1,0:T(8,128)(2,1)S(1)} %get-tuple-element.33), channel_id=1, source_target_pairs={{0,7},{1,0},{2,1},{3,2},{4,3},{5,4},{6,5},{7,6},{8,15},{9,8},{10,9... | collective-permute-start | bytes 1572872 | tf_op jit(solution)/shard_map/ppermute | solution.py:174
  50.8 10.9 %collective-permute-start.9 = (bf16[4,512,128]{2,1,0:T(8,128)(2,1)S(1)}, bf16[4,512,128]{2,1,0:T(8,128)(2,1)S(1)}, u32[]{:S(2)}, u32[]{:S(2)}) collective-permute-start(bf16[4,512,128]{2,1,0:T(8,128)(2,1)S(1)} %get-tuple-element.32), channel_id=1, source_target_pairs={{0,1},{1,2},{2,3},{3,4},{4,5},{5,6},{6,7},{7,0},{8,9},{9,10},{10,1... | collective-permute-start | bytes 1572872 | tf_op jit(solution)/shard_map/ppermute | solution.py:174
  63.0 10.1 %collective-permute-start.11 = (bf16[4,512,128]{2,1,0:T(8,128)(2,1)S(1)}, bf16[4,512,128]{2,1,0:T(8,128)(2,1)S(1)}, u32[]{:S(2)}, u32[]{:S(2)}) collective-permute-start(bf16[4,512,128]{2,1,0:T(8,128)(2,1)S(1)} %get-tuple-element.34), channel_id=1, source_target_pairs={{0,1},{1,2},{2,3},{3,4},{4,5},{5,6},{6,7},{7,0},{8,9},{9,10},{10,1... | collective-permute-start | bytes 1572872 | tf_op jit(solution)/shard_map/ppermute | solution.py:174
  63.1 10.0 %collective-permute-start.12 = (bf16[4,512,128]{2,1,0:T(8,128)(2,1)S(1)}, bf16[4,512,128]{2,1,0:T(8,128)(2,1)S(1)}, u32[]{:S(2)}, u32[]{:S(2)}) collective-permute-start(bf16[4,512,128]{2,1,0:T(8,128)(2,1)S(1)} %get-tuple-element.35), channel_id=1, source_target_pairs={{0,7},{1,0},{2,1},{3,2},{4,3},{5,4},{6,5},{7,6},{8,15},{9,8},{10,9... | collective-permute-start | bytes 1572872 | tf_op jit(solution)/shard_map/ppermute | solution.py:174
  65.7 54.1 %copy-start.4 = (f32[1,128,512]{2,1,0:T(8,128)S(1)}, f32[1,128,512]{2,1,0:T(8,128)}, u32[]{:S(2)}) copy-start(f32[1,128,512]{2,1,0:T(8,128)} %param.14) | copy-start | bytes 786436
  65.7 54.1 %copy-start.5 = (f32[1,128,512]{2,1,0:T(8,128)S(1)}, f32[1,128,512]{2,1,0:T(8,128)}, u32[]{:S(2)}) copy-start(f32[1,128,512]{2,1,0:T(8,128)} %param.13) | copy-start | bytes 786436
  65.7 54.1 %copy-start.6 = (f32[1,128,512]{2,1,0:T(8,128)S(1)}, f32[1,128,512]{2,1,0:T(8,128)}, u32[]{:S(2)}) copy-start(f32[1,128,512]{2,1,0:T(8,128)} %param.12) | copy-start | bytes 786436
  65.7 5.6 %collective-permute-start.1 = (bf16[256,512]{1,0:T(8,128)(2,1)S(1)}, bf16[256,512]{1,0:T(8,128)(2,1)S(1)}, u32[]{:S(2)}, u32[]{:S(2)}) collective-permute-start(bf16[256,512]{1,0:T(8,128)(2,1)S(1)} %get-tuple-element.24), channel_id=1, source_target_pairs={{0,8},{8,0},{1,9},{9,1},{2,10},{10,2},{3,11},{11,3},{4,12},{12,4},... | collective-permute-start | bytes 786440 | tf_op jit(solution)/shard_map/ppermute | solution.py:174
  73.8 5.7 %collective-permute-start.13 = (bf16[512,128]{1,0:T(8,128)(2,1)S(1)}, bf16[512,128]{1,0:T(8,128)(2,1)S(1)}, u32[]{:S(2)}, u32[]{:S(2)}) collective-permute-start(bf16[512,128]{1,0:T(8,128)(2,1)S(1)} %get-tuple-element.37), channel_id=1, source_target_pairs={{0,16},{16,32},{32,48},{48,0},{1,17},{17,33},{33,49},{49,1},{2,18}... | collective-permute-start | bytes 393224 | tf_op jit(solution)/shard_map/ppermute | solution.py:174
  75.3 6.2 %collective-permute-start.14 = (bf16[512,128]{1,0:T(8,128)(2,1)S(1)}, bf16[512,128]{1,0:T(8,128)(2,1)S(1)}, u32[]{:S(2)}, u32[]{:S(2)}) collective-permute-start(bf16[512,128]{1,0:T(8,128)(2,1)S(1)} %get-tuple-element.38), channel_id=1, source_target_pairs={{0,32},{16,48},{32,0},{48,16},{1,33},{17,49},{33,1},{49,17},{2,34}... | collective-permute-start | bytes 393224 | tf_op jit(solution)/shard_map/ppermute | solution.py:174
  77.7 3.8 %collective-permute-start.15 = (bf16[512,128]{1,0:T(8,128)(2,1)S(1)}, bf16[512,128]{1,0:T(8,128)(2,1)S(1)}, u32[]{:S(2)}, u32[]{:S(2)}) collective-permute-start(bf16[512,128]{1,0:T(8,128)(2,1)S(1)} %get-tuple-element.39), channel_id=1, source_target_pairs={{0,48},{16,0},{32,16},{48,32},{1,49},{17,1},{33,17},{49,33},{2,50}... | collective-permute-start | bytes 393224 | tf_op jit(solution)/shard_map/ppermute | solution.py:174
  103.0 12.4 %all-to-all-start.1 = ((f32[16,1,128]{2,1,0:T(1,128)}), f32[16,1,128]{2,1,0:T(1,128)S(1)}, u32[]{:S(2)}, u32[]{:S(2)}) async-start(f32[16,1,128]{2,1,0:T(1,128)} %broadcast_in_dim.20), calls=%async_computation.1 | async-start | bytes 16384 | tf_op jit(solution)/shard_map/all_to_all | solution.py:262
  115.5 16.4 %all-to-all-start.2 = ((bf16[16,32,512]{2,1,0:T(8,128)(2,1)}), bf16[16,32,512]{2,1,0:T(8,128)(2,1)S(1)}, u32[]{:S(2)}, u32[]{:S(2)}) async-start(bf16[16,32,512]{2,1,0:T(8,128)(2,1)} %shard_map.112), calls=%async_computation.2 | async-start | bytes 1048576 | tf_op jit(solution)/shard_map/all_to_all | solution.py:250
  120.8 11.1 %collective-permute-start.16 = (bf16[128,512]{1,0:T(8,128)(2,1)S(1)}, bf16[128,512]{1,0:T(8,128)(2,1)S(1)}, u32[]{:S(2)}, u32[]{:S(2)}) collective-permute-start(bf16[128,512]{1,0:T(8,128)(2,1)S(1)} %get-tuple-element.42), channel_id=1, source_target_pairs={{0,48},{16,0},{32,16},{48,32},{1,49},{17,1},{33,17},{49,33},{2,50}... | collective-permute-start | bytes 393224 | tf_op jit(solution)/shard_map/ppermute | solution.py:174
  121.7 10.2 %collective-permute-start.17 = (bf16[128,512]{1,0:T(8,128)(2,1)S(1)}, bf16[128,512]{1,0:T(8,128)(2,1)S(1)}, u32[]{:S(2)}, u32[]{:S(2)}) collective-permute-start(bf16[128,512]{1,0:T(8,128)(2,1)S(1)} %get-tuple-element.42), channel_id=1, source_target_pairs={{0,32},{16,48},{32,0},{48,16},{1,33},{17,49},{33,1},{49,17},{2,34}... | collective-permute-start | bytes 393224 | tf_op jit(solution)/shard_map/ppermute | solution.py:174
  122.9 9.0 %collective-permute-start.18 = (bf16[128,512]{1,0:T(8,128)(2,1)S(1)}, bf16[128,512]{1,0:T(8,128)(2,1)S(1)}, u32[]{:S(2)}, u32[]{:S(2)}) collective-permute-start(bf16[128,512]{1,0:T(8,128)(2,1)S(1)} %get-tuple-element.42), channel_id=1, source_target_pairs={{0,16},{16,32},{32,48},{48,0},{1,17},{17,33},{33,49},{49,1},{2,18}... | collective-permute-start | bytes 393224 | tf_op jit(solution)/shard_map/ppermute | solution.py:174
  (4 other events, 48.6 us)
